TPU v7x, 32 devices: a whole 2x2x4 slice. The times are simulated.
32 devices in a mesh: slab: 4 (over y, x), mem: 8 (over z, core).
Axes of the slice: x: 2, y: 2, z: 4, core: 2. Of those that a mesh axis runs over, the one named last changes fastest.
Arguments:
- ensemble: bfloat16 [1024, 32, 1024], P('mem', 'slab'), may hold values from -6 to 6
- diffusivity: float32 [32, 1024], P('slab'), may hold values from 0.05 to 0.2
- zonal_velocity: float32 [32, 1024], P('slab'), may hold values from -0.5 to 0.5
- obs_anomalies: bfloat16 [1024, 64, 128], P('mem', 'slab'), may hold values from -6 to 6
- innovations: bfloat16 [1024, 64, 128], P('mem', 'slab'), may hold values from -6 to 6
- block_lists: int32 [32, 4], P('slab'), may hold values from 0 to 15
- block_counts: int32 [32], P('slab'), may hold values from 1 to 4, 80 in all
- patch_links: int32 [32, 2], P(('slab', 'mem')), may hold values 0 or 1
Outputs:
- analysis: bfloat16 [1024, 32, 1024], P('mem', 'slab')
Inputs may be any that keep to these rules, and one draw needn't show every extreme that they name: `block_lists`: entries past a patch's count are not used. `block_counts`: some patch uses all 4 entries.
All inputs are finite; a program needn't handle non-finite values. No bound on the sum of `block_counts` or of `patch_links` on one device may be relied on, other than what follows from the above.
Results may differ from a plain program's by a relative error of at most 0.0046.
The roundings to bfloat16 on the way count: a program that leaves them out, or rounds other values in their place, can miss the bound.
Values may be sent and summed in bfloat16 or wider, within the bound.
A program may use at most 128 MiB of HBM per device.

v0:
```python
import jax
import jax.numpy as jnp
from jax import lax
from jax.sharding import PartitionSpec as P


def extended(x, sides, width):
    for axis, dim in sides:
        devices, length = (lax.axis_size(axis), x.shape[dim])
        up = [(i, (i + 1) % devices) for i in range(devices - 1)]
        down = [(j, i) for i, j in up]
        last = lax.slice_in_dim(x, length - width, length, axis=dim)
        initial = lax.slice_in_dim(x, 0, width, axis=dim)
        before = lax.ppermute(last, axis, up)
        after = lax.ppermute(initial, axis, down)
        x = jnp.concatenate([before, x, after], axis=dim)
    return x


def step_forward(members, diffusivity, zonal_velocity):
    padded = extended(members, (("slab", 1),), 1)
    values = padded[:, 1:-1, :].astype(jnp.float32)
    north_rows = padded[:, :-2, :].astype(jnp.float32)
    south_rows = padded[:, 2:, :].astype(jnp.float32)
    east_cells = jnp.roll(values, -1, axis=2)
    west_cells = jnp.roll(values, 1, axis=2)
    tendency = (
        diffusivity * (north_rows + south_rows + east_cells + west_cells - 4.0 * values)
        - zonal_velocity * (east_cells - west_cells) * 0.5
    )
    return (values + tendency).astype(jnp.bfloat16)


def listed_blocks(observed, block_lists, block_counts):
    list_width = block_lists.shape[1]
    picked = jnp.take(observed, block_lists.reshape(-1), axis=1)
    present = jnp.arange(list_width)[None, :] < block_counts[:, None]
    present = present.reshape(-1)[None, :, None]
    return jnp.where(present, picked, jnp.zeros_like(picked))


def contract_rows(left_side, right_side):
    return lax.dot_general(
        left_side, right_side, (((1,), (1,)), ((), ())), preferred_element_type=jnp.float32
    )


def patch_gain(anomaly, innovation):
    members = anomaly.shape[0]
    joined_anom = anomaly.reshape(members, -1)
    joined_innov = innovation.reshape(members, -1)
    gram_matrix = contract_rows(joined_anom, joined_anom)
    cross_term = contract_rows(joined_anom, joined_innov)
    gram_matrix = gram_matrix + (members - 1.0) * jnp.eye(members, dtype=jnp.float32)
    factor = jnp.linalg.cholesky(gram_matrix)
    halfway = lax.linalg.triangular_solve(factor, cross_term, left_side=True, lower=True)
    gain_matrix = lax.linalg.triangular_solve(
        factor, halfway, left_side=True, lower=True, transpose_a=True
    )
    return gain_matrix.astype(jnp.bfloat16)


def local(
    ensemble,
    diffusivity,
    zonal_velocity,
    obs_anomalies,
    innovations,
    block_lists,
    block_counts,
    patch_links,
):
    picked_anom = listed_blocks(obs_anomalies, block_lists, block_counts)
    picked_innov = listed_blocks(innovations, block_lists, block_counts)
    recv_anom, recv_innov = (
        lax.all_to_all(picked_anom, "mem", split_axis=1, concat_axis=0, tiled=True),
        lax.all_to_all(picked_innov, "mem", split_axis=1, concat_axis=0, tiled=True),
    )
    prior_state = step_forward(ensemble, diffusivity, zonal_velocity)
    points_leading = lax.all_to_all(prior_state, "mem", split_axis=1, concat_axis=0, tiled=True)
    patches_local = points_leading.shape[1]

    def one_patch(patch_number):
        return patch_gain(recv_anom, recv_innov)

    gains = lax.map(one_patch, jnp.arange(patches_local))
    bordered = extended(gains, ((("slab", "mem"), 0),), 1)
    link_flags = 0.5 + 0.5 * patch_links.astype(jnp.float32)
    upper_flag = link_flags[:, 0][:, None, None]
    lower_flag = link_flags[:, 1][:, None, None]
    smoothed = (
        bordered[1:-1].astype(jnp.float32)
        + upper_flag * bordered[:-2].astype(jnp.float32)
        + lower_flag * bordered[2:].astype(jnp.float32)
    )
    smoothed = (smoothed / (1.0 + upper_flag + lower_flag)).astype(jnp.bfloat16)
    update = jnp.einsum(
        "pmk,mpl->kpl", smoothed, points_leading, preferred_element_type=jnp.float32
    )
    analysed = (points_leading.astype(jnp.float32) + update).astype(jnp.bfloat16)
    return lax.all_to_all(analysed, "mem", split_axis=0, concat_axis=1, tiled=True)


def solution(mesh):
    in_specs = (
        P("mem", "slab", None),
        P("slab", None),
        P("slab", None),
        P("mem", "slab", None),
        P("mem", "slab", None),
        P("slab", None),
        P("slab"),
        P(("slab", "mem"), None),
    )
    out_specs = P("mem", "slab", None)
    return jax.shard_map(local, mesh=mesh, in_specs=in_specs, out_specs=out_specs, check_vma=False)
```

profile of v0, /device:TPU:0, one launch (start us, length us, event | category | flops | bytes accessed | tf_op | source)
XLA Modules:
  0.0 569.9 jit_solution(693474141806081478)
XLA Ops:
  1.1 4.6 gather_fusion
  5.7 4.6 gather_fusion.1
  13.2 6.4 %all-to-all-start.1 = ((bf16[128,32,128]{2,0,1:T(8,128)(2,1)}), bf16[128,32,128]{2,0,1:T(8,128)(2,1)}, u32[]{:S(2)}, u32[]{:S(2)}) async-start(bf16[128,32,128]{2,0,1:T(8,128)(2,1)} %copy.45), calls=%async_computation.1 | async-start | bytes 2097152 | tf_op jit(solution)/shard_map/all_to_all | solution.py:76
  19.6 4.9 fusion.129
  25.2 3.4 collective-permute-start
  30.1 2.7 copy.48
  32.8 4.9 fusion.126
  39.1 3.5 collective-permute-done.1
  42.6 4.8 add_convert_fusion
  47.4 4.7 all-to-all-start.2
  53.8 3.2 fusion.52
  57.0 5.5 copy.47
  62.6 4.4 fusion.2
  67.0 1.9 copy-done.4
  69.0 11.7 %cholesky.222 = f32[128,128]{1,0:T(8,128)S(1)} custom-call(f32[128,128]{1,0:T(8,128)S(1)} %cholesky.577), custom_call_target="Cholesky" | custom-call | tf_op jit(solution)/shard_map/while/body/eval_jaxpr/jit(cholesky)/cholesky | solution.py:55
  80.7 9.8 %custom-call.80 = f32[1,128,128]{1,2,0:T(8,128)S(1)} custom-call(f32[1,128,128]{2,1,0:T(8,128)S(1)} %get-tuple-element.82), custom_call_target="InvertDiagBlocksLowerTriangular" | custom-call | tf_op jit(solution)/shard_map/while/body/eval_jaxpr/jit(cholesky)/cholesky | solution.py:55
  90.5 2.5 cholesky.254
  93.0 2.4 constant_dynamic-update-slice_fusion.43
  97.0 12.1 %cholesky.243 = f32[128,128]{1,0:T(8,128)S(1)} custom-call(f32[128,128]{1,0:T(8,128)S(1)} %cholesky.581), custom_call_target="Cholesky" | custom-call | tf_op jit(solution)/shard_map/while/body/eval_jaxpr/jit(cholesky)/cholesky | solution.py:55
  109.7 9.8 %custom-call.81 = f32[1,128,128]{1,2,0:T(8,128)S(1)} custom-call(f32[1,128,128]{2,1,0:T(8,128)S(1)} %get-tuple-element.79), custom_call_target="InvertDiagBlocksLowerTriangular" | custom-call | tf_op jit(solution)/shard_map/while/body/eval_jaxpr/jit(cholesky)/cholesky | solution.py:55
  120.8 2.1 convolution_subtract_fusion.11
  122.9 11.7 %cholesky.466 = f32[128,128]{1,0:T(8,128)S(1)} custom-call(f32[128,128]{1,0:T(8,128)S(1)} %cholesky.586), custom_call_target="Cholesky" | custom-call | tf_op jit(solution)/shard_map/while/body/eval_jaxpr/jit(cholesky)/cholesky | solution.py:55
  135.9 9.8 %custom-call.82 = f32[1,128,128]{1,2,0:T(8,128)S(1)} custom-call(f32[1,128,128]{2,1,0:T(8,128)S(1)} %get-tuple-element.76), custom_call_target="InvertDiagBlocksLowerTriangular" | custom-call | tf_op jit(solution)/shard_map/while/body/eval_jaxpr/jit(cholesky)/cholesky | solution.py:55
  146.8 2.3 convolution_subtract_fusion.12
  149.2 11.9 %cholesky.485 = f32[128,128]{1,0:T(8,128)S(1)} custom-call(f32[128,128]{1,0:T(8,128)S(1)} %cholesky.591), custom_call_target="Cholesky" | custom-call | tf_op jit(solution)/shard_map/while/body/eval_jaxpr/jit(cholesky)/cholesky | solution.py:55
  162.4 9.8 %custom-call.83 = f32[1,128,128]{1,2,0:T(8,128)S(1)} custom-call(f32[1,128,128]{2,1,0:T(8,128)S(1)} %get-tuple-element.73), custom_call_target="InvertDiagBlocksLowerTriangular" | custom-call | tf_op jit(solution)/shard_map/while/body/eval_jaxpr/jit(cholesky)/cholesky | solution.py:55
  173.3 2.3 convolution_subtract_fusion.13
  175.7 11.7 %cholesky.504 = f32[128,128]{1,0:T(8,128)S(1)} custom-call(f32[128,128]{1,0:T(8,128)S(1)} %cholesky.596), custom_call_target="Cholesky" | custom-call | tf_op jit(solution)/shard_map/while/body/eval_jaxpr/jit(cholesky)/cholesky | solution.py:55
  188.7 10.0 %custom-call.84 = f32[1,128,128]{1,2,0:T(8,128)S(1)} custom-call(f32[1,128,128]{2,1,0:T(8,128)S(1)} %get-tuple-element.70), custom_call_target="InvertDiagBlocksLowerTriangular" | custom-call | tf_op jit(solution)/shard_map/while/body/eval_jaxpr/jit(cholesky)/cholesky | solution.py:55
  199.7 2.3 convolution_subtract_fusion.14
  202.0 11.7 %cholesky.524 = f32[128,128]{1,0:T(8,128)S(1)} custom-call(f32[128,128]{1,0:T(8,128)S(1)} %cholesky.601), custom_call_target="Cholesky" | custom-call | tf_op jit(solution)/shard_map/while/body/eval_jaxpr/jit(cholesky)/cholesky | solution.py:55
  215.0 9.8 %custom-call.85 = f32[1,128,128]{1,2,0:T(8,128)S(1)} custom-call(f32[1,128,128]{2,1,0:T(8,128)S(1)} %get-tuple-element.67), custom_call_target="InvertDiagBlocksLowerTriangular" | custom-call | tf_op jit(solution)/shard_map/while/body/eval_jaxpr/jit(cholesky)/cholesky | solution.py:55
  225.8 2.0 convolution_subtract_fusion.15
  227.8 12.1 %cholesky.544 = f32[128,128]{1,0:T(8,128)S(1)} custom-call(f32[128,128]{1,0:T(8,128)S(1)} %cholesky.606), custom_call_target="Cholesky" | custom-call | tf_op jit(solution)/shard_map/while/body/eval_jaxpr/jit(cholesky)/cholesky | solution.py:55
  241.2 9.8 %custom-call.86 = f32[1,128,128]{1,2,0:T(8,128)S(1)} custom-call(f32[1,128,128]{2,1,0:T(8,128)S(1)} %get-tuple-element.64), custom_call_target="InvertDiagBlocksLowerTriangular" | custom-call | tf_op jit(solution)/shard_map/while/body/eval_jaxpr/jit(cholesky)/cholesky | solution.py:55
  253.7 11.7 %cholesky.562 = f32[128,128]{1,0:T(8,128)S(1)} custom-call(f32[128,128]{1,0:T(8,128)S(1)} %convolution_subtract_fusion.16), custom_call_target="Cholesky" | custom-call | tf_op jit(solution)/shard_map/while/body/eval_jaxpr/jit(cholesky)/cholesky | solution.py:55
  272.4 4.8 select_select_fusion
  277.2 27.6 %while.1 = (s32[]{:T(128)}, f32[1024,1024]{1,0:T(8,128)}, s32[8,2]{0,1:T(2,128)S(1)}, f32[8,128,128]{2,1,0:T(8,128)}, s32[]{:T(128)}) while((s32[]{:T(128)}, f32[1024,1024]{1,0:T(8,128)}, s32[8,2]{0,1:T(2,128)S(1)}, f32[8,128,128]{2,1,0:T(8,128)}, s32[]{:T(128)}) %tuple.66), condition=%wide.while_cond, body=%wide.while_body.sunk | while | flops 2 | bytes 132705 | solution.py:57
  277.9 2.8 bitcast_dynamic-update-slice_fusion.9
  281.3 2.8 bitcast_dynamic-update-slice_fusion.9
  284.8 2.8 bitcast_dynamic-update-slice_fusion.9
  288.2 2.8 bitcast_dynamic-update-slice_fusion.9
  291.7 2.8 bitcast_dynamic-update-slice_fusion.9
  295.2 2.8 bitcast_dynamic-update-slice_fusion.9
  298.6 2.8 bitcast_dynamic-update-slice_fusion.9
  302.1 2.8 bitcast_dynamic-update-slice_fusion.9
  304.9 79.4 %custom-call.87 = f32[8,128,128]{1,2,0:T(8,128)S(1)} custom-call(f32[8,128,128]{2,1,0:T(8,128)} %get-tuple-element.25), custom_call_target="InvertDiagBlocksLowerTriangular" | custom-call | tf_op jit(solution)/shard_map/while/body/eval_jaxpr/triangular_solve | solution.py:57
  385.3 5.1 all-to-all-start
  390.4 2.6 copy.49
  393.0 3.0 fusion.48
  408.5 2.2 convolution_subtract_fusion.8
  420.9 2.1 convolution_subtract_fusion.2
  423.9 2.3 convolution_subtract_fusion.6
  432.6 3.7 collective-permute-start.2
  439.6 2.4 bitcast_convert_fusion
  442.0 5.3 copy.52
  447.4 9.2 %fusion = bf16[1024,1,1024]{0,2,1:T(8,128)(2,1)} fusion(f32[1024,1,1024]{0,2,1:T(8,128)} %copy.52, bf16[1024,1024]{1,0:T(8,128)(2,1)S(1)} %bitcast.200, bf16[1,1024,1024]{2,1,0:T(8,128)(2,1)} %collective-permute-done.3, bf16[1,1024,1024]{2,1,0:T(8,128)(2,1)} %collective-permute-done.2, bf16[1,1024,1024]{2,1,0:T(8,128)(2,1)} %bitcast_dynamic-update-slice_fusion.1, ...), kind=kOutput, calls=%fused_computation.8 | convolution fusion | flops 2159017984 | bytes 14680076 | tf_op jit(solution)/shard_map/pmk,mpl->kpl/dot_general | solution.py:97
  457.2 4.0 reduce.64
  461.1 2.6 copy.70
  463.7 6.3 %reshape.371 = bf16[8,2,65536]{2,1,0:T(2,128)(2,1)} reshape(bf16[1024,1024]{1,0:T(8,128)(2,1)} %copy.70) | data formatting | bytes 4194304
  470.0 89.8 %all_to_all.63 = bf16[8,2,65536]{2,1,0:T(2,128)(2,1)S(1)} all-to-all(bf16[8,2,65536]{2,1,0:T(2,128)(2,1)} %reshape.371), channel_id=1, replica_groups=mesh['slab'=4,'mem'=8] {'mem'}, dimensions={0} | all-to-all | bytes 4194304 | tf_op jit(solution)/shard_map/all_to_all | solution.py:101
  559.8 4.4 reshape.372
  564.2 3.1 copy.53
  567.2 2.5 copy.51
  (142 shorter events, 66.4 us)
Async XLA Ops:
  0.0 1.1 copy-start
  1.1 4.6 copy-start.2
  5.7 4.7 copy-start.9
  13.2 34.2 %all-to-all-start.1 = ((bf16[128,32,128]{2,0,1:T(8,128)(2,1)}), bf16[128,32,128]{2,0,1:T(8,128)(2,1)}, u32[]{:S(2)}, u32[]{:S(2)}) async-start(bf16[128,32,128]{2,0,1:T(8,128)(2,1)} %copy.45), calls=%async_computation.1 | async-start | bytes 2097152 | tf_op jit(solution)/shard_map/all_to_all | solution.py:76
  25.2 13.9 %collective-permute-start = (bf16[128,1,1024]{2,0,1:T(8,128)(2,1)}, bf16[128,1,1024]{2,0,1:T(8,128)(2,1)S(1)}, u32[]{:S(2)}, u32[]{:S(2)}) collective-permute-start(bf16[128,1,1024]{2,0,1:T(8,128)(2,1)} %get-tuple-element.40), channel_id=1, source_target_pairs={{0,8},{8,16},{16,24},{1,9},{9,17},{17,25},{2,10},{10,18},{18,26},{... | collective-permute-start | bytes 786440 | tf_op jit(solution)/shard_map/ppermute | solution.py:14
  28.6 14.0 %collective-permute-start.1 = (bf16[128,1,1024]{2,0,1:T(8,128)(2,1)S(1)}, bf16[128,1,1024]{2,0,1:T(8,128)(2,1)S(1)}, u32[]{:S(2)}, u32[]{:S(2)}) collective-permute-start(bf16[128,1,1024]{2,0,1:T(8,128)(2,1)S(1)} %get-tuple-element.41), channel_id=1, source_target_pairs={{8,0},{16,8},{24,16},{9,1},{17,9},{25,17},{10,2},{18,10},{26,18},{... | collective-permute-start | bytes 786440 | tf_op jit(solution)/shard_map/ppermute | solution.py:15
  32.8 9.8 %copy-start.7 = (f32[8,1024]{1,0:T(8,128)S(1)}, f32[8,1024]{1,0:T(8,128)}, u32[]{:S(2)}) copy-start(f32[8,1024]{1,0:T(8,128)} %param.12) | copy-start | bytes 98308
  32.8 9.8 %copy-start.8 = (f32[8,1024]{1,0:T(8,128)S(1)}, f32[8,1024]{1,0:T(8,128)}, u32[]{:S(2)}) copy-start(f32[8,1024]{1,0:T(8,128)} %param.11) | copy-start | bytes 98308
  47.4 336.9 %all-to-all-start.2 = ((bf16[128,32,128]{2,0,1:T(8,128)(2,1)}), bf16[128,32,128]{2,0,1:T(8,128)(2,1)S(1)}, u32[]{:S(2)}, u32[]{:S(2)}) async-start(bf16[128,32,128]{2,0,1:T(8,128)(2,1)} %copy.48), calls=%async_computation.2 | async-start | bytes 2097152 | tf_op jit(solution)/shard_map/all_to_all | solution.py:77
  53.8 3.2 copy-start.6
  67.0 1.9 copy-start.4
  384.3 1.0 copy-start.5
  385.3 54.2 %all-to-all-start = ((bf16[128,8,1024]{2,0,1:T(8,128)(2,1)}), bf16[128,8,1024]{2,0,1:T(8,128)(2,1)S(1)}, u32[]{:S(2)}, u32[]{:S(2)}) async-start(bf16[128,8,1024]{2,0,1:T(8,128)(2,1)} %add_convert_fusion), calls=%async_computation | async-start | bytes 4194304 | tf_op jit(solution)/shard_map/all_to_all | solution.py:80
  393.0 3.7 copy-start.3
  426.1 11.4 %copy-start.10 = (s32[1,2]{1,0:T(1,128)S(1)}, s32[1,2]{1,0:T(1,128)}, u32[]{:S(2)}) copy-start(s32[1,2]{1,0:T(1,128)} %param.17) | copy-start | bytes 28
  432.6 14.8 %collective-permute-start.2 = (bf16[1,1024,1024]{2,1,0:T(8,128)(2,1)}, bf16[1,1024,1024]{2,1,0:T(8,128)(2,1)}, u32[]{:S(2)}, u32[]{:S(2)}) collective-permute-start(bf16[1,1024,1024]{2,1,0:T(8,128)(2,1)} %bitcast_dynamic-update-slice_fusion.1), channel_id=1, source_target_pairs={{0,1},{1,2},{2,3},{3,4},{4,5},{5,6},{6,7},{7,8},{8,9},{9,10},{10,1... | collective-permute-start | bytes 6291464 | tf_op jit(solution)/shard_map/ppermute | solution.py:14
  436.3 11.1 %collective-permute-start.3 = (bf16[1,1024,1024]{2,1,0:T(8,128)(2,1)}, bf16[1,1024,1024]{2,1,0:T(8,128)(2,1)}, u32[]{:S(2)}, u32[]{:S(2)}) collective-permute-start(bf16[1,1024,1024]{2,1,0:T(8,128)(2,1)} %bitcast_dynamic-update-slice_fusion.1), channel_id=1, source_target_pairs={{1,0},{2,1},{3,2},{4,3},{5,4},{6,5},{7,6},{8,7},{9,8},{10,9},{11,1... | collective-permute-start | bytes 6291464 | tf_op jit(solution)/shard_map/ppermute | solution.py:15
  564.2 5.5 copy-start.1
where the time goes:
time: 578 us; the launch traced here: 570 us
  other arithmetic  283 us (49%)
  local copies, waits for them, and re-layouts  91.1 us (16%)
  blocking collectives  89.8 us (16%)
  matrix products  69 us (12%)
  starting transfers between devices  26 us (4%)
  between operations  7.32 us (1%)
    another operation x30, other arithmetic, patch_gain(): factor = jnp.linalg.cholesky(gram_matrix)  173 us
    all_to_all x1, blocking collectives, local(): lax.all_to_all(analysed, 'mem', split_axis=0, concat_axis=1, tiled=True)  89.8 us
    another operation x4, other arithmetic, patch_gain(): lax.linalg.triangular_solve(factor, halfway, left_side=True, lower=True,...  84.9 us
    another operation x24, local copies, waits for them, and re-layouts  27.6 us
    another operation x14, matrix products, patch_gain(): factor = jnp.linalg.cholesky(gram_matrix)  23.1 us
    unnamed x40, local copies, waits for them, and re-layouts  21.4 us
    another operation x15, matrix products, patch_gain(): lax.linalg.triangular_solve(factor, cross_term, left_side=True, lower=True)  15.3 us
    another operation x15, matrix products, patch_gain(): lax.linalg.triangular_solve(factor, halfway, left_side=True, lower=True,...  15.2 us
  transfers between devices with their start and end apart: 7, of which 1 were waited for; matrix products, arithmetic and copies ran while one was open for 69% of the time, Pallas kernels for 0%

commit v1 on v0

v1 whole, which is shorter than its diff:
```python
import functools

import jax
import jax.numpy as jnp
from jax import lax
from jax.experimental import pallas as pl
from jax.experimental.pallas import tpu as pltpu
from jax.sharding import PartitionSpec as P

F32, BF16 = jnp.float32, jnp.bfloat16
VMEM_SPEC = pl.BlockSpec(memory_space=pltpu.VMEM)
SMEM_SPEC = pl.BlockSpec(memory_space=pltpu.SMEM)
ANY_SPEC = pl.BlockSpec(memory_space=pl.ANY)
MESH = pl.DeviceIdType.MESH


def mm(a, b, dims, precision=None):
    return lax.dot_general(a, b, (dims, ((), ())), precision=precision, preferred_element_type=F32)


def pick_kernel(blocks, lists, counts, anom, innov, out, wide):
    patches, width = lists.shape
    members = out.shape[2]
    block = anom.shape[1]
    wide[0] = anom[...].astype(F32)
    wide[1] = innov[...].astype(F32)

    def patch(p, carry):
        for j in range(width):
            entry = lists[p, j]
            keep = (j < counts[p]).astype(F32)
            for kind in range(2):
                rows = wide[kind, pl.ds(entry, members, stride=blocks), :]
                out[p, kind, :, j * block:(j + 1) * block] = (rows * keep).astype(BF16)
        return carry

    lax.fori_loop(0, patches, patch, 0)


def pick(anom, innov, lists, counts):
    members, blocks, block = anom.shape
    patches, width = lists.shape
    return pl.pallas_call(
        functools.partial(pick_kernel, blocks),
        out_shape=jax.ShapeDtypeStruct((patches, 2, members, width * block), BF16),
        in_specs=[SMEM_SPEC, SMEM_SPEC, VMEM_SPEC, VMEM_SPEC],
        out_specs=VMEM_SPEC,
        scratch_shapes=[pltpu.VMEM((2, members * blocks, block), F32)],
    )(lists, counts, anom.reshape(-1, block), innov.reshape(-1, block))


def gain_kernel(yz, gain, a_ref, x_ref, w_ref):
    n, _, part, size = yz.shape
    members = n * part
    shift = members - 1.0
    anom = yz[:, 0].reshape(members, size)
    diag = lax.broadcasted_iota(jnp.int32, (size, size), 0) == lax.broadcasted_iota(jnp.int32, (size, size), 1)
    eye = jnp.where(diag, 1.0, 0.0).astype(F32)
    a = mm(anom, anom, ((0,), (0,))) + shift * eye
    a_ref[...] = a
    bound = jnp.max(jnp.sum(jnp.abs(a), axis=0, keepdims=True))
    start = 2.0 / (shift + bound)
    x_ref[...] = (2.0 * start) * eye - (start * start) * a

    def rough(i, carry):
        x = x_ref[...]
        xb = x.astype(BF16)
        r = eye - mm(a_ref[...].astype(BF16), xb, ((1,), (0,)))
        x_ref[...] = x + mm(xb, r.astype(BF16), ((1,), (0,)))
        return carry

    lax.fori_loop(0, 5, rough, 0)

    def norm(r):
        return jnp.max(jnp.sum(jnp.abs(r), axis=0, keepdims=True))

    def residual():
        return eye - mm(a_ref[...], x_ref[...], ((1,), (0,)), lax.Precision.HIGHEST)

    w_ref[...] = residual()
    first = norm(w_ref[...])

    @pl.when(jnp.logical_not(first < 0.5))
    def _():
        x_ref[...] = start * eye
        w_ref[...] = residual()

    def more(state):
        i, r = state
        return jnp.logical_and(i < 40, jnp.logical_not(r < 0.004))

    def refine(state):
        i, _ = state
        x_ref[...] += mm(x_ref[...], w_ref[...], ((1,), (0,)), lax.Precision.HIGHEST)
        w_ref[...] = residual()
        return i + 1, norm(w_ref[...])

    lax.while_loop(more, refine, (jnp.int32(0), jnp.where(first < 0.5, first, 1.0)))
    x_ref[...] += mm(x_ref[...], w_ref[...], ((1,), (0,)), lax.Precision.HIGHEST)

    x = x_ref[...]
    xh = x.astype(BF16)
    xl = (x - xh.astype(F32)).astype(BF16)
    innov = yz[:, 1].reshape(members, size)
    step = min(256, members)
    for i in range(members // step):
        rows = anom[i * step:(i + 1) * step]
        w = mm(rows, xh, ((1,), (0,))) + mm(rows, xl, ((1,), (0,)))
        wh = w.astype(BF16)
        wl = (w - wh.astype(F32)).astype(BF16)
        g = mm(wh, innov, ((1,), (1,))) + mm(wl, innov, ((1,), (1,)))
        gain[i * step:(i + 1) * step, :] = g.astype(BF16)


def patch_gain(yz):
    n, _, part, size = yz.shape
    members = n * part
    return pl.pallas_call(
        gain_kernel,
        out_shape=jax.ShapeDtypeStruct((members, members), BF16),
        in_specs=[VMEM_SPEC],
        out_specs=VMEM_SPEC,
        scratch_shapes=[pltpu.VMEM((size, size), F32)] * 3,
        cost_estimate=pl.CostEstimate(flops=40 * 10**9, bytes_accessed=4 * 10**6, transcendentals=0),
    )(yz)


def update_kernel(n, links, own, before, after, prior, out, ready, send_sem, recv_sem, local_sem):
    me = lax.axis_index("mem")
    members, points = prior.shape
    part = members // n
    chunk = max(part, min(128, members))
    inside = chunk // part
    chunks = members // chunk
    barrier = pltpu.get_barrier_semaphore()

    def greet(s, carry):
        pl.semaphore_signal(barrier, inc=1, device_id={"mem": lax.rem(me + s, n)}, device_id_type=MESH)
        return carry

    lax.fori_loop(1, n, greet, 0)
    pl.semaphore_wait(barrier, n - 1)

    up = 0.5 + 0.5 * links[0, 0].astype(F32)
    low = 0.5 + 0.5 * links[0, 1].astype(F32)
    scale = 1.0 + up + low

    def copy(d):
        return pltpu.make_async_remote_copy(
            src_ref=ready.at[d], dst_ref=out.at[me], send_sem=send_sem.at[d], recv_sem=recv_sem.at[me],
            device_id={"mem": d}, device_id_type=MESH)

    keep = pltpu.make_async_copy(ready.at[me], out.at[me], local_sem)

    def piece(s, carry):
        c = lax.rem(me // inside + s + 1, chunks)
        cols = pl.ds(pl.multiple_of(c * chunk, chunk), chunk)
        smooth = own[:, cols].astype(F32) + up * before[:, cols].astype(F32) + low * after[:, cols].astype(F32)
        smooth = (smooth / scale).astype(BF16)
        new = mm(smooth, prior[...], ((0,), (0,)))
        new = (prior[cols, :].astype(F32) + new).astype(BF16)
        for i in range(inside):
            d = c * inside + i
            ready[d] = new[i * part:(i + 1) * part, :]

            @pl.when(d != me)
            def _():
                copy(d).start()
        return carry

    lax.fori_loop(0, chunks, piece, 0)
    keep.start()

    def finish(s, carry):
        d = lax.rem(me + s, n)
        copy(d).wait_send()
        pltpu.make_async_remote_copy(
            src_ref=ready.at[d], dst_ref=out.at[d], send_sem=send_sem.at[d], recv_sem=recv_sem.at[d],
            device_id={"mem": d}, device_id_type=MESH).wait_recv()
        return carry

    lax.fori_loop(1, n, finish, 0)
    keep.wait()


def update(links, own, before, after, prior, n):
    members, points = prior.shape
    part = members // n
    return pl.pallas_call(
        functools.partial(update_kernel, n),
        out_shape=jax.ShapeDtypeStruct((n, part, points), BF16),
        in_specs=[SMEM_SPEC] + [VMEM_SPEC] * 4,
        out_specs=ANY_SPEC,
        scratch_shapes=[
            pltpu.VMEM((n, part, points), BF16),
            pltpu.SemaphoreType.DMA((n,)),
            pltpu.SemaphoreType.DMA((n,)),
            pltpu.SemaphoreType.DMA,
        ],
        compiler_params=pltpu.CompilerParams(collective_id=0, has_side_effects=True),
        cost_estimate=pl.CostEstimate(flops=2 * members * members * points, bytes_accessed=10**7, transcendentals=0),
    )(links, own, before, after, prior)


def shifted(x, axis, by):
    count = lax.axis_size(axis)
    pairs = [(i, i + by) for i in range(count) if 0 <= i + by < count]
    return lax.ppermute(x, axis, pairs)


def forecast(ensemble, diffusivity, zonal_velocity):
    rows = jnp.transpose(ensemble, (1, 0, 2))
    before = shifted(rows[-1:], "slab", 1)
    after = shifted(rows[:1], "slab", -1)
    padded = jnp.concatenate([before, rows, after], axis=0)
    values = rows.astype(F32)
    north, south = padded[:-2].astype(F32), padded[2:].astype(F32)
    east, west = jnp.roll(values, -1, axis=2), jnp.roll(values, 1, axis=2)
    tendency = diffusivity[:, None, :] * (north + south + east + west - 4.0 * values) - zonal_velocity[:, None, :] * (east - west) * 0.5
    return (values + tendency).astype(BF16)


def local(ensemble, diffusivity, zonal_velocity, obs_anomalies, innovations, block_lists, block_counts, patch_links):
    n = lax.axis_size("mem")
    swap = functools.partial(lax.all_to_all, axis_name="mem", split_axis=0, concat_axis=0, tiled=True)
    yz = swap(pick(obs_anomalies, innovations, block_lists, block_counts))
    prior = swap(forecast(ensemble, diffusivity, zonal_velocity))
    prior = prior.reshape(-1, prior.shape[-1])
    gain = patch_gain(yz)
    before = shifted(gain, ("slab", "mem"), 1)
    after = shifted(gain, ("slab", "mem"), -1)
    out = update(patch_links, gain, before, after, prior, n)
    return jnp.transpose(out, (1, 0, 2))


def solution(mesh):
    in_specs = (
        P("mem", "slab", None),
        P("slab", None),
        P("slab", None),
        P("mem", "slab", None),
        P("mem", "slab", None),
        P("slab", None),
        P("slab"),
        P(("slab", "mem"), None),
    )
    return jax.shard_map(local, mesh=mesh, in_specs=in_specs, out_specs=P("mem", "slab", None), check_vma=False)
```

time: 578 us -> 223 us (0.39)
  the two profiles are of different devices: /device:TPU:0 before, /device:TPU:11 now
where the time goes in v1:
time: 223 us
  waiting for transfers between devices  98.1 us (44%)
  Pallas kernels  84.8 us (38%)
  starting transfers between devices  23.2 us (10%)
  local copies, waits for them, and re-layouts  8.65 us (4%)
  other arithmetic  7.91 us (4%)
    pallas_call x1, Pallas kernels, update(): pl.pallas_call(functools.partial(update_kernel, n), out_shape=jax.ShapeDt...  60.6 us
    ppermute x4, waiting for transfers between devices, shifted(): return lax.ppermute(x, axis, pairs)  55.5 us
    all_to_all x1, waiting for transfers between devices, local(): yz = swap(pick(obs_anomalies, innovations, block_lists, block_counts))  21.6 us
    all_to_all x1, waiting for transfers between devices, local(): prior = swap(forecast(ensemble, diffusivity, zonal_velocity))  21 us
    pallas_call x1, Pallas kernels, patch_gain(): pl.pallas_call(gain_kernel, out_shape=jax.ShapeDtypeStruct((members, memb...  19.3 us
    ppermute x4, starting transfers between devices, shifted(): return lax.ppermute(x, axis, pairs)  10.6 us
    all_to_all x1, starting transfers between devices, local(): prior = swap(forecast(ensemble, diffusivity, zonal_velocity))  7.02 us
    all_to_all x1, starting transfers between devices, local(): yz = swap(pick(obs_anomalies, innovations, block_lists, block_counts))  5.6 us
  transfers between devices with their start and end apart: 6, of which 6 were waited for; matrix products, arithmetic and copies ran while one was open for 4% of the time, Pallas kernels for 9%

profile of v1, /device:TPU:11, one launch (start us, length us, event | category | flops | bytes accessed | tf_op | source)
XLA Modules:
  0.0 222.8 jit_solution(3107018580500600064)
XLA Ops:
  0.0 1.3 copy.12.lists
  1.3 4.9 %shard_map.82 = bf16[8,2,128,512]{3,2,1,0:T(8,128)(2,1)} custom-call(s32[8,4]{1,0:T(8,128)} %copy.12.lists, s32[8]{0:T(128)} %counts.1, bf16[2048,128]{1,0:T(8,128)(2,1)} %bitcast.10, bf16[2048,128]{1,0:T(8,128)(2,1)} %bitcast.11), custom_call_target="tpu_custom_call" | custom-call | tf_op jit(solution)/shard_map/pallas_call | solution.py:43
  6.2 5.6 %all-to-all-start = ((bf16[8,2,128,512]{3,2,1,0:T(8,128)(2,1)}), bf16[8,2,128,512]{3,2,1,0:T(8,128)(2,1)S(1)}, u32[]{:S(2)}, u32[]{:S(2)}) async-start(bf16[8,2,128,512]{3,2,1,0:T(8,128)(2,1)} %shard_map.82), calls=%async_computation | async-start | bytes 4194304 | tf_op jit(solution)/shard_map/all_to_all | solution.py:226
  11.8 3.0 %copy_bitcast_fusion = (bf16[8,128,1024]{2,1,0:T(8,128)(2,1)S(1)}, f32[8,128,1024]{2,1,0:T(8,128)S(1)}) fusion(bf16[128,8,1024]{2,1,0:T(8,128)(2,1)} %param.8), kind=kLoop, calls=%fused_computation.5 | loop fusion | flops 1048576 | bytes 8388608 | tf_op jit(solution)/shard_map/transpose | solution.py:212
  14.9 3.1 %collective-permute-start.2 = (bf16[1,128,1024]{2,1,0:T(8,128)(2,1)S(1)}, bf16[1,128,1024]{2,1,0:T(8,128)(2,1)S(1)}, u32[]{:S(2)}, u32[]{:S(2)}) collective-permute-start(bf16[1,128,1024]{2,1,0:T(8,128)(2,1)S(1)} %get-tuple-element.9), channel_id=1, source_target_pairs={{0,8},{8,16},{16,24},{1,9},{9,17},{17,25},{2,10},{10,18},{18,26},{... | collective-permute-start | bytes 786440 | tf_op jit(solution)/shard_map/ppermute | solution.py:208
  18.0 2.2 collective-permute-start.3
  20.2 0.0 copy-start.2
  20.2 0.0 copy-start.3
  20.2 1.7 fusion.1
  21.9 0.2 fusion.2
  22.1 2.1 collective-permute-done.2
  24.3 6.6 %collective-permute-done.3 = bf16[1,128,1024]{2,1,0:T(8,128)(2,1)S(1)} collective-permute-done((bf16[1,128,1024]{2,1,0:T(8,128)(2,1)S(1)}, bf16[1,128,1024]{2,1,0:T(8,128)(2,1)S(1)}, u32[]{:S(2)}, u32[]{:S(2)}) %collective-permute-start.3) | collective-permute-done | bytes 262176 | tf_op jit(solution)/shard_map/ppermute | solution.py:208
  30.8 0.0 copy-done.2
  30.8 0.0 copy-done.3
  30.8 4.9 %add_convert_fusion = bf16[8,128,1024]{2,1,0:T(8,128)(2,1)} fusion(f32[8,128,1023]{2,1,0:T(8,128)S(1)} %get-tuple-element.6, f32[8,128,1]{2,1,0:T(8,128)S(1)} %get-tuple-element.8, f32[8,128,1]{2,1,0:T(8,128)S(1)} %get-tuple-element.7, f32[8,128,1023]{2,1,0:T(8,128)S(1)} %get-tuple-element.5, bf16[1,128,1024]{2,1,0:T(8,128)(2,1)S(1)} %collective-permute-done.3, ...), kind=kLoop, calls=%fused_computation.2 | loop fusion | flops 19922944 | bytes 13172736 | tf_op jit(solution)/shard_map/convert_element_type | solution.py:220
  35.7 21.6 %all-to-all-done.yz = bf16[8,2,128,512]{3,2,1,0:T(8,128)(2,1)S(1)} async-done(((bf16[8,2,128,512]{3,2,1,0:T(8,128)(2,1)}), bf16[8,2,128,512]{3,2,1,0:T(8,128)(2,1)S(1)}, u32[]{:S(2)}, u32[]{:S(2)}) %all-to-all-start) | async-done | bytes 2097184 | tf_op jit(solution)/shard_map/all_to_all | solution.py:226
  57.4 0.0 copy-start.1
  57.4 1.3 copy-done.1
  58.7 7.0 %all-to-all-start.1 = ((bf16[8,128,1024]{2,1,0:T(8,128)(2,1)}), bf16[8,128,1024]{2,1,0:T(8,128)(2,1)S(1)}, u32[]{:S(2)}, u32[]{:S(2)}) async-start(bf16[8,128,1024]{2,1,0:T(8,128)(2,1)} %add_convert_fusion), calls=%async_computation.1 | async-start | bytes 4194304 | tf_op jit(solution)/shard_map/all_to_all | solution.py:227
  65.7 19.3 %shard_map.83.own = bf16[1024,1024]{1,0:T(8,128)(2,1)} custom-call(bf16[8,2,128,512]{3,2,1,0:T(8,128)(2,1)} %copy-done.1), custom_call_target="tpu_custom_call" | custom-call | flops 40000000000 | bytes 4000000 | tf_op jit(solution)/shard_map/pallas_call | solution.py:118
  85.0 3.4 %collective-permute-start = (bf16[1024,1024]{1,0:T(8,128)(2,1)}, bf16[1024,1024]{1,0:T(8,128)(2,1)}, u32[]{:S(2)}, u32[]{:S(2)}) collective-permute-start(bf16[1024,1024]{1,0:T(8,128)(2,1)} %shard_map.83.own), channel_id=1, source_target_pairs={{0,1},{1,2},{2,3},{3,4},{4,5},{5,6},{6,7},{7,8},{8,9},{9,10},{10,1... | collective-permute-start | bytes 6291464 | tf_op jit(solution)/shard_map/ppermute | solution.py:208
  88.4 1.9 collective-permute-start.1
  90.3 21.0 %all-to-all-done.1 = bf16[8,128,1024]{2,1,0:T(8,128)(2,1)S(1)} async-done(((bf16[8,128,1024]{2,1,0:T(8,128)(2,1)}), bf16[8,128,1024]{2,1,0:T(8,128)(2,1)S(1)}, u32[]{:S(2)}, u32[]{:S(2)}) %all-to-all-start.1) | async-done | bytes 2097184 | tf_op jit(solution)/shard_map/all_to_all | solution.py:227
  111.3 0.0 copy-start
  111.3 45.0 %collective-permute-done.before = bf16[1024,1024]{1,0:T(8,128)(2,1)} collective-permute-done((bf16[1024,1024]{1,0:T(8,128)(2,1)}, bf16[1024,1024]{1,0:T(8,128)(2,1)}, u32[]{:S(2)}, u32[]{:S(2)}) %collective-permute-start) | collective-permute-done | bytes 2097184 | tf_op jit(solution)/shard_map/ppermute | solution.py:208
  156.3 1.8 collective-permute-done.1.after
  158.1 0.0 copy-done
  158.1 60.6 %shard_map.84 = bf16[8,128,1024]{2,1,0:T(8,128)(2,1)} custom-call(s32[1,2]{1,0:T(1,128)} %links.1, bf16[1024,1024]{1,0:T(8,128)(2,1)} %shard_map.83.own, bf16[1024,1024]{1,0:T(8,128)(2,1)} %collective-permute-done.before, bf16[1024,1024]{1,0:T(8,128)(2,1)} %collective-permute-done.1.after, bf16[1024,1024]{1,0:T(8,128)(2,1)} %bitcast.8), custom_call_target="tpu_custom_call" | custom-call | flops 2147483648 | bytes 10000000 | tf_op jit(solution)/shard_map/pallas_call | solution.py:189
  218.7 4.1 %copy.14 = bf16[128,8,1024]{2,1,0:T(8,128)(2,1)} copy(bf16[128,8,1024]{2,0,1:T(8,128)(2,1)} %bitcast.9) | data formatting | bytes 4194304 | tf_op jit(solution)/shard_map/transpose | solution.py:233
  (1 shorter events, 0.0 us)
Async XLA Ops:
  6.2 51.1 %all-to-all-start = ((bf16[8,2,128,512]{3,2,1,0:T(8,128)(2,1)}), bf16[8,2,128,512]{3,2,1,0:T(8,128)(2,1)S(1)}, u32[]{:S(2)}, u32[]{:S(2)}) async-start(bf16[8,2,128,512]{3,2,1,0:T(8,128)(2,1)} %shard_map.82), calls=%async_computation | async-start | bytes 4194304 | tf_op jit(solution)/shard_map/all_to_all | solution.py:226
  14.9 9.4 %collective-permute-start.2 = (bf16[1,128,1024]{2,1,0:T(8,128)(2,1)S(1)}, bf16[1,128,1024]{2,1,0:T(8,128)(2,1)S(1)}, u32[]{:S(2)}, u32[]{:S(2)}) collective-permute-start(bf16[1,128,1024]{2,1,0:T(8,128)(2,1)S(1)} %get-tuple-element.9), channel_id=1, source_target_pairs={{0,8},{8,16},{16,24},{1,9},{9,17},{17,25},{2,10},{10,18},{18,26},{... | collective-permute-start | bytes 786440 | tf_op jit(solution)/shard_map/ppermute | solution.py:208
  18.0 12.8 %collective-permute-start.3 = (bf16[1,128,1024]{2,1,0:T(8,128)(2,1)S(1)}, bf16[1,128,1024]{2,1,0:T(8,128)(2,1)S(1)}, u32[]{:S(2)}, u32[]{:S(2)}) collective-permute-start(bf16[1,128,1024]{2,1,0:T(8,128)(2,1)S(1)} %get-tuple-element.10), channel_id=1, source_target_pairs={{8,0},{16,8},{24,16},{9,1},{17,9},{25,17},{10,2},{18,10},{26,18},{... | collective-permute-start | bytes 786440 | tf_op jit(solution)/shard_map/ppermute | solution.py:208
  20.2 10.6 %copy-start.2 = (f32[8,1024]{1,0:T(8,128)S(1)}, f32[8,1024]{1,0:T(8,128)}, u32[]{:S(2)}) copy-start(f32[8,1024]{1,0:T(8,128)} %param.10) | copy-start | bytes 98308
  20.2 10.6 %copy-start.3 = (f32[8,1024]{1,0:T(8,128)S(1)}, f32[8,1024]{1,0:T(8,128)}, u32[]{:S(2)}) copy-start(f32[8,1024]{1,0:T(8,128)} %param.9) | copy-start | bytes 98308
  57.4 1.3 copy-start.1
  58.7 52.6 %all-to-all-start.1 = ((bf16[8,128,1024]{2,1,0:T(8,128)(2,1)}), bf16[8,128,1024]{2,1,0:T(8,128)(2,1)S(1)}, u32[]{:S(2)}, u32[]{:S(2)}) async-start(bf16[8,128,1024]{2,1,0:T(8,128)(2,1)} %add_convert_fusion), calls=%async_computation.1 | async-start | bytes 4194304 | tf_op jit(solution)/shard_map/all_to_all | solution.py:227
  85.0 71.3 %collective-permute-start = (bf16[1024,1024]{1,0:T(8,128)(2,1)}, bf16[1024,1024]{1,0:T(8,128)(2,1)}, u32[]{:S(2)}, u32[]{:S(2)}) collective-permute-start(bf16[1024,1024]{1,0:T(8,128)(2,1)} %shard_map.83.own), channel_id=1, source_target_pairs={{0,1},{1,2},{2,3},{3,4},{4,5},{5,6},{6,7},{7,8},{8,9},{9,10},{10,1... | collective-permute-start | bytes 6291464 | tf_op jit(solution)/shard_map/ppermute | solution.py:208
  88.4 69.7 %collective-permute-start.1 = (bf16[1024,1024]{1,0:T(8,128)(2,1)}, bf16[1024,1024]{1,0:T(8,128)(2,1)}, u32[]{:S(2)}, u32[]{:S(2)}) collective-permute-start(bf16[1024,1024]{1,0:T(8,128)(2,1)} %shard_map.83.own), channel_id=1, source_target_pairs={{1,0},{2,1},{3,2},{4,3},{5,4},{6,5},{7,6},{8,7},{9,8},{10,9},{11,1... | collective-permute-start | bytes 6291464 | tf_op jit(solution)/shard_map/ppermute | solution.py:208
  111.3 46.8 %copy-start = (bf16[8,128,1024]{2,1,0:T(8,128)(2,1)}, bf16[8,128,1024]{2,1,0:T(8,128)(2,1)S(1)}, u32[]{:S(2)}) copy-start(bf16[8,128,1024]{2,1,0:T(8,128)(2,1)S(1)} %all-to-all-done.1) | copy-start | bytes 6291460

commit v2 on v1

--- a/solution.py
+++ b/solution.py
@@ -18,20 +18,31 @@
     return lax.dot_general(a, b, (dims, ((), ())), precision=precision, preferred_element_type=F32)
 
 
+def turned(index, count):
+    odd = lax.rem(lax.axis_index("slab"), 2)
+    return index + odd * (count - 1 - 2 * index)
+
+
+def holder(patch, count):
+    slab, index = divmod(patch, count)
+    return slab * count + (index if slab % 2 == 0 else count - 1 - index)
+
+
 def pick_kernel(blocks, lists, counts, anom, innov, out, wide):
-    patches, width = lists.shape
+    width, patches = lists.shape
     members = out.shape[2]
     block = anom.shape[1]
     wide[0] = anom[...].astype(F32)
     wide[1] = innov[...].astype(F32)
 
-    def patch(p, carry):
+    def patch(slot, carry):
+        p = turned(slot, patches)
         for j in range(width):
-            entry = lists[p, j]
+            entry = lists[j, p]
             keep = (j < counts[p]).astype(F32)
             for kind in range(2):
                 rows = wide[kind, pl.ds(entry, members, stride=blocks), :]
-                out[p, kind, :, j * block:(j + 1) * block] = (rows * keep).astype(BF16)
+                out[slot, kind, :, j * block:(j + 1) * block] = (rows * keep).astype(BF16)
         return carry
 
     lax.fori_loop(0, patches, patch, 0)
@@ -46,7 +57,7 @@
         in_specs=[SMEM_SPEC, SMEM_SPEC, VMEM_SPEC, VMEM_SPEC],
         out_specs=VMEM_SPEC,
         scratch_shapes=[pltpu.VMEM((2, members * blocks, block), F32)],
-    )(lists, counts, anom.reshape(-1, block), innov.reshape(-1, block))
+    )(lists.T, counts, anom.reshape(-1, block), innov.reshape(-1, block))
 
 
 def gain_kernel(yz, gain, a_ref, x_ref, w_ref):
@@ -132,6 +143,9 @@
     chunk = max(part, min(128, members))
     inside = chunk // part
     chunks = members // chunk
+    half = chunks // 2
+    mine, place = me // inside // half, lax.rem(me // inside, half)
+    row = turned(me, n)
     barrier = pltpu.get_barrier_semaphore()
 
     def greet(s, carry):
@@ -147,13 +161,15 @@
 
     def copy(d):
         return pltpu.make_async_remote_copy(
-            src_ref=ready.at[d], dst_ref=out.at[me], send_sem=send_sem.at[d], recv_sem=recv_sem.at[me],
+            src_ref=ready.at[d], dst_ref=out.at[row], send_sem=send_sem.at[d], recv_sem=recv_sem.at[me],
             device_id={"mem": d}, device_id_type=MESH)
 
-    keep = pltpu.make_async_copy(ready.at[me], out.at[me], local_sem)
+    keep = pltpu.make_async_copy(ready.at[me], out.at[row], local_sem)
 
     def piece(s, carry):
-        c = lax.rem(me // inside + s + 1, chunks)
+        near = s // half
+        side = mine + (1 - near) * (1 - 2 * mine)
+        c = side * half + lax.rem(place + s + near, half)
         cols = pl.ds(pl.multiple_of(c * chunk, chunk), chunk)
         smooth = own[:, cols].astype(F32) + up * before[:, cols].astype(F32) + low * after[:, cols].astype(F32)
         smooth = (smooth / scale).astype(BF16)
@@ -175,7 +191,7 @@
         d = lax.rem(me + s, n)
         copy(d).wait_send()
         pltpu.make_async_remote_copy(
-            src_ref=ready.at[d], dst_ref=out.at[d], send_sem=send_sem.at[d], recv_sem=recv_sem.at[d],
+            src_ref=ready.at[d], dst_ref=out.at[turned(d, n)], send_sem=send_sem.at[d], recv_sem=recv_sem.at[d],
             device_id={"mem": d}, device_id_type=MESH).wait_recv()
         return carry
 
@@ -208,12 +224,21 @@
     return lax.ppermute(x, axis, pairs)
 
 
+def neighbour(x, slabs, count, by):
+    total = slabs * count
+    pairs = [(holder(p, count), holder(p + by, count)) for p in range(total) if 0 <= p + by < total]
+    return lax.ppermute(x, ("slab", "mem"), pairs)
+
+
 def forecast(ensemble, diffusivity, zonal_velocity):
     rows = jnp.transpose(ensemble, (1, 0, 2))
     before = shifted(rows[-1:], "slab", 1)
     after = shifted(rows[:1], "slab", -1)
     padded = jnp.concatenate([before, rows, after], axis=0)
-    values = rows.astype(F32)
+    odd = lax.rem(lax.axis_index("slab"), 2) == 1
+    padded, diffusivity, zonal_velocity = (
+        jnp.where(odd, x[::-1], x) for x in (padded, diffusivity, zonal_velocity))
+    values = padded[1:-1].astype(F32)
     north, south = padded[:-2].astype(F32), padded[2:].astype(F32)
     east, west = jnp.roll(values, -1, axis=2), jnp.roll(values, 1, axis=2)
     tendency = diffusivity[:, None, :] * (north + south + east + west - 4.0 * values) - zonal_velocity[:, None, :] * (east - west) * 0.5
@@ -227,9 +252,11 @@
     prior = swap(forecast(ensemble, diffusivity, zonal_velocity))
     prior = prior.reshape(-1, prior.shape[-1])
     gain = patch_gain(yz)
-    before = shifted(gain, ("slab", "mem"), 1)
-    after = shifted(gain, ("slab", "mem"), -1)
-    out = update(patch_links, gain, before, after, prior, n)
+    slabs = lax.axis_size("slab")
+    before = neighbour(gain, slabs, n, 1)
+    after = neighbour(gain, slabs, n, -1)
+    links = lax.ppermute(patch_links, ("slab", "mem"), [(i, holder(i, n)) for i in range(slabs * n)])
+    out = update(links, gain, before, after, prior, n)
     return jnp.transpose(out, (1, 0, 2))
 
 

time: 223 us -> 200 us (0.90)
  the two profiles are of different devices: /device:TPU:11 before, /device:TPU:0 now
where the time goes in v2:
time: 200 us
  Pallas kernels  110 us (55%)
  waiting for transfers between devices  54.8 us (27%)
  starting transfers between devices  19.4 us (10%)
  local copies, waits for them, and re-layouts  10.4 us (5%)
  other arithmetic  5.96 us (3%)
    pallas_call x1, Pallas kernels, update(): pl.pallas_call(functools.partial(update_kernel, n), out_shape=jax.ShapeDt...  81.5 us
    pallas_call x1, Pallas kernels, patch_gain(): pl.pallas_call(gain_kernel, out_shape=jax.ShapeDtypeStruct((members, memb...  23.1 us
    all_to_all x1, waiting for transfers between devices, local(): prior = swap(forecast(ensemble, diffusivity, zonal_velocity))  21.4 us
    all_to_all x1, waiting for transfers between devices, local(): yz = swap(pick(obs_anomalies, innovations, block_lists, block_counts))  21.3 us
    ppermute x2, waiting for transfers between devices, shifted(): return lax.ppermute(x, axis, pairs)  12.1 us
    all_to_all x1, starting transfers between devices, local(): yz = swap(pick(obs_anomalies, innovations, block_lists, block_counts))  6.49 us
    pallas_call x1, Pallas kernels, pick(): pl.pallas_call(functools.partial(pick_kernel, blocks), out_shape=jax.Shap...  4.99 us
    ppermute x2, starting transfers between devices, shifted(): return lax.ppermute(x, axis, pairs)  4.7 us
  transfers between devices with their start and end apart: 7, of which 4 were waited for; matrix products, arithmetic and copies ran while one was open for 5% of the time, Pallas kernels for 12%

profile of v2, /device:TPU:0, one launch (start us, length us, event | category | flops | bytes accessed | tf_op | source)
XLA Modules:
  0.0 200.2 jit_solution(5376691369988535018)
XLA Ops:
  0.0 5.0 %shard_map.82 = bf16[8,2,128,512]{3,2,1,0:T(8,128)(2,1)} custom-call(s32[4,8]{1,0:T(4,128)} %bitcast.14, s32[8]{0:T(128)} %counts.1, bf16[2048,128]{1,0:T(8,128)(2,1)} %bitcast.12, bf16[2048,128]{1,0:T(8,128)(2,1)} %bitcast.13), custom_call_target="tpu_custom_call" | custom-call | tf_op jit(solution)/shard_map/pallas_call | solution.py:54
  5.0 0.0 copy-start.2
  5.0 0.0 copy-start.1
  5.0 6.5 %all-to-all-start = ((bf16[8,2,128,512]{3,2,1,0:T(8,128)(2,1)}), bf16[8,2,128,512]{3,2,1,0:T(8,128)(2,1)}, u32[]{:S(2)}, u32[]{:S(2)}) async-start(bf16[8,2,128,512]{3,2,1,0:T(8,128)(2,1)} %shard_map.82), calls=%async_computation | async-start | bytes 4194304 | tf_op jit(solution)/shard_map/all_to_all | solution.py:251
  11.5 2.7 %copy.14 = bf16[128,8,1024]{2,0,1:T(8,128)(2,1)S(1)} copy(bf16[128,8,1024]{2,1,0:T(8,128)(2,1)} %param.8) | data formatting | bytes 4194304 | tf_op args[0]
  14.3 3.4 %collective-permute-start.3 = (bf16[1,128,1024]{2,1,0:T(8,128)(2,1)S(1)}, bf16[1,128,1024]{2,1,0:T(8,128)(2,1)S(1)}, u32[]{:S(2)}, u32[]{:S(2)}) collective-permute-start(bf16[1,128,1024]{2,1,0:T(8,128)(2,1)S(1)} %get-tuple-element.9), channel_id=1, source_target_pairs={{0,8},{8,16},{16,24},{1,9},{9,17},{17,25},{2,10},{10,18},{18,26},{... | collective-permute-start | bytes 786440 | tf_op jit(solution)/shard_map/ppermute | solution.py:224
  17.7 1.3 collective-permute-start.4
  19.0 0.0 copy-done.2
  19.0 0.2 rev.10
  19.2 0.0 copy-done.1
  19.2 0.2 rev.11
  19.4 4.5 %collective-permute-done.3 = bf16[1,128,1024]{2,1,0:T(8,128)(2,1)S(1)} collective-permute-done((bf16[1,128,1024]{2,1,0:T(8,128)(2,1)S(1)}, bf16[1,128,1024]{2,1,0:T(8,128)(2,1)S(1)}, u32[]{:S(2)}, u32[]{:S(2)}) %collective-permute-start.3) | collective-permute-done | bytes 262176 | tf_op jit(solution)/shard_map/ppermute | solution.py:224
  23.9 7.6 %collective-permute-done.4 = bf16[1,128,1024]{2,1,0:T(8,128)(2,1)S(1)} collective-permute-done((bf16[1,128,1024]{2,1,0:T(8,128)(2,1)S(1)}, bf16[1,128,1024]{2,1,0:T(8,128)(2,1)S(1)}, u32[]{:S(2)}, u32[]{:S(2)}) %collective-permute-start.4) | collective-permute-done | bytes 262176 | tf_op jit(solution)/shard_map/ppermute | solution.py:224
  31.5 0.3 pad_maximum_fusion.2
  31.8 0.8 reverse_select_fusion
  32.6 0.5 slice_convert_fusion
  33.1 0.2 fusion.1
  33.3 1.7 fusion
  34.9 4.4 %add_convert_fusion = bf16[8,128,1024]{2,1,0:T(8,128)(2,1)} fusion(f32[8,128,1023]{2,1,0:T(8,128)S(1)} %get-tuple-element.6, f32[8,128,1]{2,1,0:T(8,128)S(1)} %get-tuple-element.8, f32[8,128,1]{2,1,0:T(8,128)S(1)} %get-tuple-element.7, f32[8,128,1023]{2,1,0:T(8,128)S(1)} %get-tuple-element.5, bf16[10,128,1024]{2,1,0:T(8,128)(2,1)S(1)} %reverse_select_fusion, ...), kind=kLoop, calls=%fused_computation.2 | loop fusion | flops 17825792 | bytes 16842752 | tf_op jit(solution)/shard_map/convert_element_type | solution.py:245
  39.3 21.3 %all-to-all-done.yz = bf16[8,2,128,512]{3,2,1,0:T(8,128)(2,1)} async-done(((bf16[8,2,128,512]{3,2,1,0:T(8,128)(2,1)}), bf16[8,2,128,512]{3,2,1,0:T(8,128)(2,1)}, u32[]{:S(2)}, u32[]{:S(2)}) %all-to-all-start) | async-done | bytes 2097184 | tf_op jit(solution)/shard_map/all_to_all | solution.py:251
  60.6 3.6 %all-to-all-start.1 = ((bf16[8,128,1024]{2,1,0:T(8,128)(2,1)}), bf16[8,128,1024]{2,1,0:T(8,128)(2,1)S(1)}, u32[]{:S(2)}, u32[]{:S(2)}) async-start(bf16[8,128,1024]{2,1,0:T(8,128)(2,1)} %add_convert_fusion), calls=%async_computation.1 | async-start | bytes 4194304 | tf_op jit(solution)/shard_map/all_to_all | solution.py:252
  64.2 0.0 copy-start.4
  64.2 23.1 %shard_map.83.own = bf16[1024,1024]{1,0:T(8,128)(2,1)} custom-call(bf16[8,2,128,512]{3,2,1,0:T(8,128)(2,1)} %all-to-all-done.yz), custom_call_target="tpu_custom_call" | custom-call | flops 40000000000 | bytes 4000000 | tf_op jit(solution)/shard_map/pallas_call | solution.py:129
  87.3 2.6 %collective-permute-start.1 = (bf16[1024,1024]{1,0:T(8,128)(2,1)}, bf16[1024,1024]{1,0:T(8,128)(2,1)}, u32[]{:S(2)}, u32[]{:S(2)}) collective-permute-start(bf16[1024,1024]{1,0:T(8,128)(2,1)} %shard_map.83.own), channel_id=1, source_target_pairs={{0,1},{1,2},{2,3},{3,4},{4,5},{5,6},{6,7},{7,15},{15,14},{14,13},{... | collective-permute-start | bytes 6291464 | tf_op jit(solution)/shard_map/ppermute | solution.py:230
  89.9 1.3 collective-permute-start.2
  91.2 0.0 copy-done.4
  91.2 0.7 collective-permute-start
  91.9 0.0 collective-permute-done.links
  91.9 0.0 copy-start.3
  91.9 21.4 %all-to-all-done.1 = bf16[8,128,1024]{2,1,0:T(8,128)(2,1)S(1)} async-done(((bf16[8,128,1024]{2,1,0:T(8,128)(2,1)}), bf16[8,128,1024]{2,1,0:T(8,128)(2,1)S(1)}, u32[]{:S(2)}, u32[]{:S(2)}) %all-to-all-start.1) | async-done | bytes 2097184 | tf_op jit(solution)/shard_map/all_to_all | solution.py:252
  113.3 0.0 copy-start
  113.3 0.0 collective-permute-done.1.before
  113.3 0.0 collective-permute-done.2.after
  113.3 0.0 copy-done.3
  113.3 1.3 copy-done
  114.6 81.5 %shard_map.84 = bf16[8,128,1024]{2,1,0:T(8,128)(2,1)} custom-call(s32[1,2]{1,0:T(1,128)} %copy-done.3, bf16[1024,1024]{1,0:T(8,128)(2,1)} %shard_map.83.own, bf16[1024,1024]{1,0:T(8,128)(2,1)} %collective-permute-done.1.before, bf16[1024,1024]{1,0:T(8,128)(2,1)} %collective-permute-done.2.after, bf16[1024,1024]{1,0:T(8,128)(2,1)} %bitcast.10), custom_call_target="tpu_custom_call" | custom-call | flops 2147483648 | bytes 10000000 | tf_op jit(solution)/shard_map/pallas_call | solution.py:205
  196.2 4.1 %copy.12 = bf16[128,8,1024]{2,1,0:T(8,128)(2,1)} copy(bf16[128,8,1024]{2,0,1:T(8,128)(2,1)} %bitcast.11) | data formatting | bytes 4194304 | tf_op jit(solution)/shard_map/transpose | solution.py:260
  (2 shorter events, 0.0 us)
Async XLA Ops:
  5.0 14.0 %copy-start.2 = (f32[8,1024]{1,0:T(8,128)S(1)}, f32[8,1024]{1,0:T(8,128)}, u32[]{:S(2)}) copy-start(f32[8,1024]{1,0:T(8,128)} %param.9) | copy-start | bytes 98308
  5.0 14.2 %copy-start.1 = (f32[8,1024]{1,0:T(8,128)S(1)}, f32[8,1024]{1,0:T(8,128)}, u32[]{:S(2)}) copy-start(f32[8,1024]{1,0:T(8,128)} %param.10) | copy-start | bytes 98308
  5.0 55.6 %all-to-all-start = ((bf16[8,2,128,512]{3,2,1,0:T(8,128)(2,1)}), bf16[8,2,128,512]{3,2,1,0:T(8,128)(2,1)}, u32[]{:S(2)}, u32[]{:S(2)}) async-start(bf16[8,2,128,512]{3,2,1,0:T(8,128)(2,1)} %shard_map.82), calls=%async_computation | async-start | bytes 4194304 | tf_op jit(solution)/shard_map/all_to_all | solution.py:251
  14.3 9.6 %collective-permute-start.3 = (bf16[1,128,1024]{2,1,0:T(8,128)(2,1)S(1)}, bf16[1,128,1024]{2,1,0:T(8,128)(2,1)S(1)}, u32[]{:S(2)}, u32[]{:S(2)}) collective-permute-start(bf16[1,128,1024]{2,1,0:T(8,128)(2,1)S(1)} %get-tuple-element.9), channel_id=1, source_target_pairs={{0,8},{8,16},{16,24},{1,9},{9,17},{17,25},{2,10},{10,18},{18,26},{... | collective-permute-start | bytes 786440 | tf_op jit(solution)/shard_map/ppermute | solution.py:224
  17.7 13.8 %collective-permute-start.4 = (bf16[1,128,1024]{2,1,0:T(8,128)(2,1)S(1)}, bf16[1,128,1024]{2,1,0:T(8,128)(2,1)S(1)}, u32[]{:S(2)}, u32[]{:S(2)}) collective-permute-start(bf16[1,128,1024]{2,1,0:T(8,128)(2,1)S(1)} %get-tuple-element.10), channel_id=1, source_target_pairs={{8,0},{16,8},{24,16},{9,1},{17,9},{25,17},{10,2},{18,10},{26,18},{... | collective-permute-start | bytes 786440 | tf_op jit(solution)/shard_map/ppermute | solution.py:224
  60.6 52.7 %all-to-all-start.1 = ((bf16[8,128,1024]{2,1,0:T(8,128)(2,1)}), bf16[8,128,1024]{2,1,0:T(8,128)(2,1)S(1)}, u32[]{:S(2)}, u32[]{:S(2)}) async-start(bf16[8,128,1024]{2,1,0:T(8,128)(2,1)} %add_convert_fusion), calls=%async_computation.1 | async-start | bytes 4194304 | tf_op jit(solution)/shard_map/all_to_all | solution.py:252
  64.2 27.0 %copy-start.4 = (s32[1,2]{1,0:T(1,128)S(1)}, s32[1,2]{1,0:T(1,128)}, u32[]{:S(2)}) copy-start(s32[1,2]{1,0:T(1,128)} %param.15) | copy-start | bytes 28
  87.3 26.0 %collective-permute-start.1 = (bf16[1024,1024]{1,0:T(8,128)(2,1)}, bf16[1024,1024]{1,0:T(8,128)(2,1)}, u32[]{:S(2)}, u32[]{:S(2)}) collective-permute-start(bf16[1024,1024]{1,0:T(8,128)(2,1)} %shard_map.83.own), channel_id=1, source_target_pairs={{0,1},{1,2},{2,3},{3,4},{4,5},{5,6},{6,7},{7,15},{15,14},{14,13},{... | collective-permute-start | bytes 6291464 | tf_op jit(solution)/shard_map/ppermute | solution.py:230
  89.9 23.4 %collective-permute-start.2 = (bf16[1024,1024]{1,0:T(8,128)(2,1)}, bf16[1024,1024]{1,0:T(8,128)(2,1)}, u32[]{:S(2)}, u32[]{:S(2)}) collective-permute-start(bf16[1024,1024]{1,0:T(8,128)(2,1)} %shard_map.83.own), channel_id=1, source_target_pairs={{1,0},{2,1},{3,2},{4,3},{5,4},{6,5},{7,6},{15,7},{14,15},{13,14},{... | collective-permute-start | bytes 6291464 | tf_op jit(solution)/shard_map/ppermute | solution.py:230
  91.2 0.7 collective-permute-start
  91.9 21.4 %copy-start.3 = (s32[1,2]{1,0:T(1,128)}, s32[1,2]{1,0:T(1,128)S(1)}, u32[]{:S(2)}) copy-start(s32[1,2]{1,0:T(1,128)S(1)} %collective-permute-done.links) | copy-start | bytes 28
  113.3 1.4 copy-start

commit v3 on v2

v3 whole, which is shorter than its diff:
```python
import functools

import jax
import jax.numpy as jnp
from jax import lax
from jax.experimental import pallas as pl
from jax.experimental.pallas import tpu as pltpu
from jax.sharding import PartitionSpec as P

F32, BF16 = jnp.float32, jnp.bfloat16
VMEM_SPEC = pl.BlockSpec(memory_space=pltpu.VMEM)
SMEM_SPEC = pl.BlockSpec(memory_space=pltpu.SMEM)
ANY_SPEC = pl.BlockSpec(memory_space=pl.ANY)
MESH = pl.DeviceIdType.MESH


def mm(a, b, dims, precision=None):
    return lax.dot_general(a, b, (dims, ((), ())), precision=precision, preferred_element_type=F32)


def turned(index, count):
    odd = lax.rem(lax.axis_index("slab"), 2)
    return index + odd * (count - 1 - 2 * index)


def holder(patch, count):
    slab, index = divmod(patch, count)
    return slab * count + (index if slab % 2 == 0 else count - 1 - index)


def pick_kernel(blocks, lists, counts, anom, innov, first, second, wide):
    width, patches = lists.shape
    members = first.shape[1]
    block = anom.shape[1]
    wide[0] = anom[...].astype(F32)
    wide[1] = innov[...].astype(F32)

    def patch(slot, carry):
        p = turned(slot, patches)
        for j in range(width):
            entry = lists[j, p]
            keep = (j < counts[p]).astype(F32)
            for kind, out in enumerate((first, second)):
                rows = wide[kind, pl.ds(entry, members, stride=blocks), :]
                out[slot, :, j * block:(j + 1) * block] = (rows * keep).astype(BF16)
        return carry

    lax.fori_loop(0, patches, patch, 0)


def pick(anom, innov, lists, counts):
    members, blocks, block = anom.shape
    patches, width = lists.shape
    return pl.pallas_call(
        functools.partial(pick_kernel, blocks),
        out_shape=[jax.ShapeDtypeStruct((patches, members, width * block), BF16)] * 2,
        in_specs=[SMEM_SPEC, SMEM_SPEC, VMEM_SPEC, VMEM_SPEC],
        out_specs=[VMEM_SPEC] * 2,
        scratch_shapes=[pltpu.VMEM((2, members * blocks, block), F32)],
    )(lists.T, counts, anom.reshape(-1, block), innov.reshape(-1, block))


def weight_kernel(anom, weight, a_ref, x_ref, w_ref):
    members, size = anom.shape
    shift = members - 1.0
    diag = lax.broadcasted_iota(jnp.int32, (size, size), 0) == lax.broadcasted_iota(jnp.int32, (size, size), 1)
    eye = jnp.where(diag, 1.0, 0.0).astype(F32)
    a = mm(anom[...], anom[...], ((0,), (0,))) + shift * eye
    a_ref[...] = a
    bound = jnp.max(jnp.sum(jnp.abs(a), axis=0, keepdims=True))
    start = 2.0 / (shift + bound)
    x_ref[...] = (2.0 * start) * eye - (start * start) * a

    def rough(i, carry):
        x = x_ref[...]
        xb = x.astype(BF16)
        r = eye - mm(a_ref[...].astype(BF16), xb, ((1,), (0,)))
        x_ref[...] = x + mm(xb, r.astype(BF16), ((1,), (0,)))
        return carry

    lax.fori_loop(0, 5, rough, 0)

    def norm(r):
        return jnp.max(jnp.sum(jnp.abs(r), axis=0, keepdims=True))

    def residual():
        return eye - mm(a_ref[...], x_ref[...], ((1,), (0,)), lax.Precision.HIGHEST)

    w_ref[...] = residual()
    first = norm(w_ref[...])

    @pl.when(jnp.logical_not(first < 0.5))
    def _():
        x_ref[...] = start * eye
        w_ref[...] = residual()

    def more(state):
        i, r = state
        return jnp.logical_and(i < 40, jnp.logical_not(r < 0.004))

    def refine(state):
        i, _ = state
        x_ref[...] += mm(x_ref[...], w_ref[...], ((1,), (0,)), lax.Precision.HIGHEST)
        w_ref[...] = residual()
        return i + 1, norm(w_ref[...])

    lax.while_loop(more, refine, (jnp.int32(0), jnp.where(first < 0.5, first, 1.0)))
    x_ref[...] += mm(x_ref[...], w_ref[...], ((1,), (0,)), lax.Precision.HIGHEST)

    x = x_ref[...]
    xh = x.astype(BF16)
    xl = (x - xh.astype(F32)).astype(BF16)
    step = min(256, members)
    for i in range(members // step):
        rows = anom[i * step:(i + 1) * step]
        w = mm(rows, xh, ((1,), (0,))) + mm(rows, xl, ((1,), (0,)))
        wh = w.astype(BF16)
        weight[0, i * step:(i + 1) * step, :] = wh
        weight[1, i * step:(i + 1) * step, :] = (w - wh.astype(F32)).astype(BF16)


def patch_weight(anom):
    members, size = anom.shape
    return pl.pallas_call(
        weight_kernel,
        out_shape=jax.ShapeDtypeStruct((2, members, size), BF16),
        in_specs=[VMEM_SPEC],
        out_specs=VMEM_SPEC,
        scratch_shapes=[pltpu.VMEM((size, size), F32)] * 3,
        cost_estimate=pl.CostEstimate(flops=20 * 10**9, bytes_accessed=4 * 10**6, transcendentals=0),
    )(anom)


def update_kernel(n, slabs, links, weight, innov, states, out, prior, own, before, after, ready,
                  send_f, recv_f, send_g, recv_g, send_d, recv_d, local_sem):
    me, slab = lax.axis_index("mem"), lax.axis_index("slab")
    members, points = prior.shape
    part = members // n
    chunks, _, chunk = own.shape
    inside = chunk // part
    half = chunks // 2
    mine, place = me // inside // half, lax.rem(me // inside, half)
    row = turned(me, n)
    way = 1 - 2 * lax.rem(slab, 2)
    last, first = row // (n - 1), (n - 1 - row) // (n - 1)
    following = {"slab": slab + last, "mem": me + way * (1 - last)}
    previous = {"slab": slab - first, "mem": me - way * (1 - first)}
    total, number = slabs * n, slab * n + row
    has_next, has_prev = number < total - 1, number > 0
    edge_next = last * (1 - slab // (slabs - 1))
    edge_prev = first * (1 - (slabs - 1 - slab) // (slabs - 1))

    barrier = pltpu.get_barrier_semaphore()

    def greet(s, carry):
        pl.semaphore_signal(barrier, inc=1, device_id={"slab": slab, "mem": lax.rem(me + s, n)}, device_id_type=MESH)
        return carry

    lax.fori_loop(1, n, greet, 0)
    for edge, other in ((edge_next, following), (edge_prev, previous)):
        @pl.when(edge == 1)
        def _():
            pl.semaphore_signal(barrier, inc=1, device_id=other, device_id_type=MESH)

    pl.semaphore_wait(barrier, n - 1 + edge_next + edge_prev)

    def span(d):
        return pl.ds(pl.multiple_of(d * part, part), part)

    def remote(src, dst, send, recv, device):
        return pltpu.make_async_remote_copy(
            src_ref=src, dst_ref=dst, send_sem=send, recv_sem=recv, device_id=device, device_id_type=MESH)

    def peer(d):
        return {"slab": slab, "mem": d}

    def far_first(s):
        near = s // half
        side = mine + (1 - near) * (1 - 2 * mine)
        return side * half + lax.rem(place + s + near, half)

    def send_states(s, carry):
        c = far_first(s)
        for i in range(inside):
            d = c * inside + i

            @pl.when(d != me)
            def _():
                remote(states.at[d], prior.at[span(me)], send_f.at[d], recv_f.at[me], peer(d)).start()
        return carry

    lax.fori_loop(0, chunks, send_states, 0)
    prior[span(me), :] = states[me]

    def to_next(c):
        return remote(own.at[c], before.at[c], send_g.at[0, c], recv_g.at[0, c], following)

    def to_prev(c):
        return remote(own.at[c], after.at[c], send_g.at[1, c], recv_g.at[1, c], previous)

    def gains(s, carry):
        c = far_first(s)
        rows = innov[pl.ds(pl.multiple_of(c * chunk, chunk), chunk), :]
        own[c] = (mm(weight[0], rows, ((1,), (1,))) + mm(weight[1], rows, ((1,), (1,)))).astype(BF16)

        @pl.when(has_next)
        def _():
            to_next(c).start()

        @pl.when(has_prev)
        def _():
            to_prev(c).start()
        return carry

    lax.fori_loop(0, chunks, gains, 0)

    @pl.when(jnp.logical_not(has_prev))
    def _():
        before[...] = jnp.zeros_like(before)

    @pl.when(jnp.logical_not(has_next))
    def _():
        after[...] = jnp.zeros_like(after)

    up = 0.5 + 0.5 * links[0, 0].astype(F32)
    low = 0.5 + 0.5 * links[0, 1].astype(F32)
    scale = 1.0 + up + low

    def states_came(s, carry):
        d = lax.rem(me + s, n)
        remote(states.at[d], prior.at[span(d)], send_f.at[d], recv_f.at[d], peer(d)).wait()
        return carry

    lax.fori_loop(1, n, states_came, 0)

    def copy(d):
        return remote(ready.at[d], out.at[row], send_d.at[d], recv_d.at[me], peer(d))

    keep = pltpu.make_async_copy(ready.at[me], out.at[row], local_sem)

    def piece(s, carry):
        c = far_first(s)

        @pl.when(has_next)
        def _():
            to_prev_twin = remote(own.at[c], after.at[c], send_g.at[0, c], recv_g.at[1, c], following)
            to_prev_twin.wait()

        @pl.when(has_prev)
        def _():
            to_next_twin = remote(own.at[c], before.at[c], send_g.at[1, c], recv_g.at[0, c], previous)
            to_next_twin.wait()

        smooth = own[c].astype(F32) + up * before[c].astype(F32) + low * after[c].astype(F32)
        smooth = (smooth / scale).astype(BF16)
        new = mm(smooth, prior[...], ((0,), (0,)))
        rows = prior[pl.ds(pl.multiple_of(c * chunk, chunk), chunk), :]
        new = (rows.astype(F32) + new).astype(BF16)
        for i in range(inside):
            d = c * inside + i
            ready[d] = new[i * part:(i + 1) * part, :]

            @pl.when(d != me)
            def _():
                copy(d).start()
        return carry

    lax.fori_loop(0, chunks, piece, 0)
    keep.start()

    def finish(s, carry):
        d = lax.rem(me + s, n)
        remote(ready.at[d], out.at[turned(d, n)], send_d.at[d], recv_d.at[d], peer(d)).wait()
        return carry

    lax.fori_loop(1, n, finish, 0)
    keep.wait()


def update(links, weight, innov, states, slabs):
    n, part, points = states.shape
    members = n * part
    chunk = max(part, min(128, members))
    gains = pltpu.VMEM((members // chunk, members, chunk), BF16)
    return pl.pallas_call(
        functools.partial(update_kernel, n, slabs),
        out_shape=jax.ShapeDtypeStruct((n, part, points), BF16),
        in_specs=[SMEM_SPEC] + [VMEM_SPEC] * 3,
        out_specs=ANY_SPEC,
        scratch_shapes=[pltpu.VMEM((members, points), BF16), gains, gains, gains, pltpu.VMEM((n, part, points), BF16)]
        + [pltpu.SemaphoreType.DMA((n,))] * 2
        + [pltpu.SemaphoreType.DMA((2, members // chunk))] * 2
        + [pltpu.SemaphoreType.DMA((n,))] * 2
        + [pltpu.SemaphoreType.DMA],
        compiler_params=pltpu.CompilerParams(collective_id=0, has_side_effects=True),
        cost_estimate=pl.CostEstimate(flops=2 * members * members * points, bytes_accessed=10**7, transcendentals=0),
    )(links, weight, innov, states)


def shifted(x, axis, by):
    count = lax.axis_size(axis)
    pairs = [(i, i + by) for i in range(count) if 0 <= i + by < count]
    return lax.ppermute(x, axis, pairs)


def forecast(ensemble, diffusivity, zonal_velocity):
    rows = jnp.transpose(ensemble, (1, 0, 2))
    before = shifted(rows[-1:], "slab", 1)
    after = shifted(rows[:1], "slab", -1)
    padded = jnp.concatenate([before, rows, after], axis=0)
    odd = lax.rem(lax.axis_index("slab"), 2) == 1
    padded, diffusivity, zonal_velocity = (
        jnp.where(odd, x[::-1], x) for x in (padded, diffusivity, zonal_velocity))
    values = padded[1:-1].astype(F32)
    north, south = padded[:-2].astype(F32), padded[2:].astype(F32)
    east, west = jnp.roll(values, -1, axis=2), jnp.roll(values, 1, axis=2)
    tendency = diffusivity[:, None, :] * (north + south + east + west - 4.0 * values) - zonal_velocity[:, None, :] * (east - west) * 0.5
    return (values + tendency).astype(BF16)


def local(ensemble, diffusivity, zonal_velocity, obs_anomalies, innovations, block_lists, block_counts, patch_links):
    n = lax.axis_size("mem")
    swap = functools.partial(lax.all_to_all, axis_name="mem", split_axis=0, concat_axis=0, tiled=True)
    slabs = lax.axis_size("slab")
    links = lax.ppermute(patch_links, ("slab", "mem"), [(i, holder(i, n)) for i in range(slabs * n)])
    anom, innov = pick(obs_anomalies, innovations, block_lists, block_counts)
    states = forecast(ensemble, diffusivity, zonal_velocity)
    anom = swap(anom)
    anom, innov = lax.optimization_barrier((anom, innov))
    innov = swap(innov)
    size = anom.shape[-1]
    weight = patch_weight(anom.reshape(-1, size))
    out = update(links, weight, innov.reshape(-1, size), states, slabs)
    return jnp.transpose(out, (1, 0, 2))


def solution(mesh):
    in_specs = (
        P("mem", "slab", None),
        P("slab", None),
        P("slab", None),
        P("mem", "slab", None),
        P("mem", "slab", None),
        P("slab", None),
        P("slab"),
        P(("slab", "mem"), None),
    )
    return jax.shard_map(local, mesh=mesh, in_specs=in_specs, out_specs=P("mem", "slab", None), check_vma=False)
```

time: 200 us -> 223 us (1.11)
  the two profiles are of different devices: /device:TPU:0 before, /device:TPU:5 now
where the time goes in v3:
time: 223 us; the launch traced here: 221 us
  Pallas kernels  161 us (72%)
  waiting for transfers between devices  24.9 us (11%)
  starting transfers between devices  17.4 us (8%)
  local copies, waits for them, and re-layouts  10.8 us (5%)
  other arithmetic  6.9 us (3%)
    pallas_call x1, Pallas kernels, update(): pl.pallas_call(functools.partial(update_kernel, n, slabs), out_shape=jax....  139 us
    pallas_call x1, Pallas kernels, patch_weight(): pl.pallas_call(weight_kernel, out_shape=jax.ShapeDtypeStruct((2, members,...  16.4 us
    all_to_all x1, waiting for transfers between devices, local(): anom = swap(anom)  15.7 us
    all_to_all x1, waiting for transfers between devices, local(): innov = swap(innov)  9.19 us
    ppermute x2, starting transfers between devices, shifted(): return lax.ppermute(x, axis, pairs)  6.17 us
    all_to_all x1, starting transfers between devices, local(): anom = swap(anom)  6.11 us
    pallas_call x1, Pallas kernels, pick(): pl.pallas_call(functools.partial(pick_kernel, blocks), out_shape=[jax.Sha...  4.98 us
  transfers between devices with their start and end apart: 5, of which 2 were waited for; matrix products, arithmetic and copies ran while one was open for 4% of the time, Pallas kernels for 10%

profile of v3, /device:TPU:5, one launch (start us, length us, event | category | flops | bytes accessed | tf_op | source)
XLA Modules:
  0.0 220.8 jit_solution(2433308152383531991)
XLA Ops:
  0.0 0.0 copy-start.4
  0.0 0.0 copy-start.3
  0.0 0.0 copy-start.2
  0.0 2.8 %copy.12 = bf16[128,8,1024]{2,0,1:T(8,128)(2,1)S(1)} copy(bf16[128,8,1024]{2,1,0:T(8,128)(2,1)} %param.8) | data formatting | bytes 4194304 | tf_op args[0]
  2.8 0.8 fusion.2
  3.6 3.1 %collective-permute-start.1 = (bf16[1,128,1024]{2,1,0:T(8,128)(2,1)}, bf16[1,128,1024]{2,1,0:T(8,128)(2,1)S(1)}, u32[]{:S(2)}, u32[]{:S(2)}) collective-permute-start(bf16[1,128,1024]{2,1,0:T(8,128)(2,1)} %get-tuple-element.17), channel_id=1, source_target_pairs={{0,8},{8,16},{16,24},{1,9},{9,17},{17,25},{2,10},{10,18},{18,26},{... | collective-permute-start | bytes 786440 | tf_op jit(solution)/shard_map/ppermute | solution.py:303
  6.7 3.1 %collective-permute-start.2 = (bf16[1,128,1024]{2,1,0:T(8,128)(2,1)}, bf16[1,128,1024]{2,1,0:T(8,128)(2,1)}, u32[]{:S(2)}, u32[]{:S(2)}) collective-permute-start(bf16[1,128,1024]{2,1,0:T(8,128)(2,1)} %get-tuple-element.18), channel_id=1, source_target_pairs={{8,0},{16,8},{24,16},{9,1},{17,9},{25,17},{10,2},{18,10},{26,18},{... | collective-permute-start | bytes 786440 | tf_op jit(solution)/shard_map/ppermute | solution.py:303
  9.8 5.0 %shard_map.82 = (bf16[8,128,512]{2,1,0:T(8,128)(2,1)}, bf16[8,128,512]{2,1,0:T(8,128)(2,1)}) custom-call(s32[4,8]{1,0:T(4,128)} %bitcast.16, s32[8]{0:T(128)} %counts.1, bf16[2048,128]{1,0:T(8,128)(2,1)} %bitcast.14, bf16[2048,128]{1,0:T(8,128)(2,1)} %bitcast.15), custom_call_target="tpu_custom_call" | custom-call | tf_op jit(solution)/shard_map/pallas_call | solution.py:54
  14.8 6.1 %all-to-all-start = ((bf16[8,128,512]{2,1,0:T(8,128)(2,1)}), bf16[8,128,512]{2,1,0:T(8,128)(2,1)S(1)}, u32[]{:S(2)}, u32[]{:S(2)}) async-start(bf16[8,128,512]{2,1,0:T(8,128)(2,1)} %get-tuple-element.9), calls=%async_computation | async-start | bytes 2097152 | tf_op jit(solution)/shard_map/all_to_all | solution.py:328
  20.9 0.0 copy-done.4
  20.9 0.7 collective-permute-start
  21.6 0.0 copy-done.3
  21.6 0.2 rev.10
  21.7 0.0 copy-done.2
  21.7 0.2 rev.11
  21.9 0.0 collective-permute-done.1
  21.9 0.0 collective-permute-done.2
  21.9 1.3 pad_maximum_fusion.2
  23.2 0.8 reverse_select_fusion
  24.0 0.5 slice_convert_fusion
  24.5 0.2 fusion.1
  24.7 1.7 fusion
  26.4 4.4 %add_convert_fusion.states = bf16[8,128,1024]{2,1,0:T(8,128)(2,1)} fusion(f32[8,128,1023]{2,1,0:T(8,128)S(1)} %get-tuple-element.14, f32[8,128,1]{2,1,0:T(8,128)S(1)} %get-tuple-element.16, f32[8,128,1]{2,1,0:T(8,128)S(1)} %get-tuple-element.15, f32[8,128,1023]{2,1,0:T(8,128)S(1)} %get-tuple-element.13, bf16[10,128,1024]{2,1,0:T(8,128)(2,1)S(1)} %reverse_select_fusion, ...), kind=kLoop, calls=%fused_computation.2 | loop fusion | flops 17825792 | bytes 16842752 | tf_op jit(solution)/shard_map/convert_element_type | solution.py:318
  30.7 15.7 %all-to-all-done = bf16[8,128,512]{2,1,0:T(8,128)(2,1)S(1)} async-done(((bf16[8,128,512]{2,1,0:T(8,128)(2,1)}), bf16[8,128,512]{2,1,0:T(8,128)(2,1)S(1)}, u32[]{:S(2)}, u32[]{:S(2)}) %all-to-all-start) | async-done | bytes 1048608 | tf_op jit(solution)/shard_map/all_to_all | solution.py:328
  46.5 0.0 copy-start
  46.5 4.4 %all-to-all-start.1 = ((bf16[8,128,512]{2,1,0:T(8,128)(2,1)}), bf16[8,128,512]{2,1,0:T(8,128)(2,1)S(1)}, u32[]{:S(2)}, u32[]{:S(2)}) async-start(bf16[8,128,512]{2,1,0:T(8,128)(2,1)} %get-tuple-element.12), calls=%async_computation.1 | async-start | bytes 2097152 | tf_op jit(solution)/shard_map/all_to_all | solution.py:330
  50.9 0.0 copy-done
  50.9 16.4 %shard_map.83.weight = bf16[2,1024,512]{2,1,0:T(8,128)(2,1)} custom-call(bf16[1024,512]{1,0:T(8,128)(2,1)} %bitcast.12), custom_call_target="tpu_custom_call" | custom-call | flops 20000000000 | bytes 4000000 | tf_op jit(solution)/shard_map/pallas_call | solution.py:124
  67.4 0.0 collective-permute-done.links
  67.4 0.0 copy-start.5
  67.4 9.2 %all-to-all-done.1 = bf16[8,128,512]{2,1,0:T(8,128)(2,1)S(1)} async-done(((bf16[8,128,512]{2,1,0:T(8,128)(2,1)}), bf16[8,128,512]{2,1,0:T(8,128)(2,1)S(1)}, u32[]{:S(2)}, u32[]{:S(2)}) %all-to-all-start.1) | async-done | bytes 1048608 | tf_op jit(solution)/shard_map/all_to_all | solution.py:330
  76.5 0.0 copy-start.1
  76.5 0.0 copy-done.5
  76.5 1.0 copy-done.1
  77.5 139.2 %shard_map.84 = bf16[8,128,1024]{2,1,0:T(8,128)(2,1)} custom-call(s32[1,2]{1,0:T(1,128)} %copy-done.5, bf16[2,1024,512]{2,1,0:T(8,128)(2,1)} %shard_map.83.weight, bf16[1024,512]{1,0:T(8,128)(2,1)} %bitcast.13, bf16[8,128,1024]{2,1,0:T(8,128)(2,1)} %add_convert_fusion.states), custom_call_target="tpu_custom_call" | custom-call | flops 2147483648 | bytes 10000000 | tf_op jit(solution)/shard_map/pallas_call | solution.py:285
  216.8 4.1 %copy.10 = bf16[128,8,1024]{2,1,0:T(8,128)(2,1)} copy(bf16[128,8,1024]{2,0,1:T(8,128)(2,1)} %bitcast.11) | data formatting | bytes 4194304 | tf_op jit(solution)/shard_map/transpose | solution.py:334
  (1 shorter events, 0.0 us)
Async XLA Ops:
  0.0 20.9 %copy-start.4 = (s32[1,2]{1,0:T(1,128)S(1)}, s32[1,2]{1,0:T(1,128)}, u32[]{:S(2)}) copy-start(s32[1,2]{1,0:T(1,128)} %param.15) | copy-start | bytes 28
  0.0 21.6 %copy-start.3 = (f32[8,1024]{1,0:T(8,128)S(1)}, f32[8,1024]{1,0:T(8,128)}, u32[]{:S(2)}) copy-start(f32[8,1024]{1,0:T(8,128)} %param.9) | copy-start | bytes 98308
  0.0 21.7 %copy-start.2 = (f32[8,1024]{1,0:T(8,128)S(1)}, f32[8,1024]{1,0:T(8,128)}, u32[]{:S(2)}) copy-start(f32[8,1024]{1,0:T(8,128)} %param.10) | copy-start | bytes 98308
  3.6 18.3 %collective-permute-start.1 = (bf16[1,128,1024]{2,1,0:T(8,128)(2,1)}, bf16[1,128,1024]{2,1,0:T(8,128)(2,1)S(1)}, u32[]{:S(2)}, u32[]{:S(2)}) collective-permute-start(bf16[1,128,1024]{2,1,0:T(8,128)(2,1)} %get-tuple-element.17), channel_id=1, source_target_pairs={{0,8},{8,16},{16,24},{1,9},{9,17},{17,25},{2,10},{10,18},{18,26},{... | collective-permute-start | bytes 786440 | tf_op jit(solution)/shard_map/ppermute | solution.py:303
  6.7 15.2 %collective-permute-start.2 = (bf16[1,128,1024]{2,1,0:T(8,128)(2,1)}, bf16[1,128,1024]{2,1,0:T(8,128)(2,1)}, u32[]{:S(2)}, u32[]{:S(2)}) collective-permute-start(bf16[1,128,1024]{2,1,0:T(8,128)(2,1)} %get-tuple-element.18), channel_id=1, source_target_pairs={{8,0},{16,8},{24,16},{9,1},{17,9},{25,17},{10,2},{18,10},{26,18},{... | collective-permute-start | bytes 786440 | tf_op jit(solution)/shard_map/ppermute | solution.py:303
  14.8 31.7 %all-to-all-start = ((bf16[8,128,512]{2,1,0:T(8,128)(2,1)}), bf16[8,128,512]{2,1,0:T(8,128)(2,1)S(1)}, u32[]{:S(2)}, u32[]{:S(2)}) async-start(bf16[8,128,512]{2,1,0:T(8,128)(2,1)} %get-tuple-element.9), calls=%async_computation | async-start | bytes 2097152 | tf_op jit(solution)/shard_map/all_to_all | solution.py:328
  20.9 46.5 %collective-permute-start = (s32[1,2]{1,0:T(1,128)S(1)}, s32[1,2]{1,0:T(1,128)S(1)}, u32[]{:S(2)}, u32[]{:S(2)}) collective-permute-start(s32[1,2]{1,0:T(1,128)S(1)} %copy-done.4), channel_id=1, source_target_pairs={{0,0},{1,1},{2,2},{3,3},{4,4},{5,5},{6,6},{7,7},{8,15},{9,14},{10,... | collective-permute-start | bytes 32 | tf_op jit(solution)/shard_map/ppermute | solution.py:325
  46.5 4.4 %copy-start = (bf16[8,128,512]{2,1,0:T(8,128)(2,1)}, bf16[8,128,512]{2,1,0:T(8,128)(2,1)S(1)}, u32[]{:S(2)}) copy-start(bf16[8,128,512]{2,1,0:T(8,128)(2,1)S(1)} %all-to-all-done) | copy-start | bytes 3145732
  46.5 30.1 %all-to-all-start.1 = ((bf16[8,128,512]{2,1,0:T(8,128)(2,1)}), bf16[8,128,512]{2,1,0:T(8,128)(2,1)S(1)}, u32[]{:S(2)}, u32[]{:S(2)}) async-start(bf16[8,128,512]{2,1,0:T(8,128)(2,1)} %get-tuple-element.12), calls=%async_computation.1 | async-start | bytes 2097152 | tf_op jit(solution)/shard_map/all_to_all | solution.py:330
  67.4 9.2 %copy-start.5 = (s32[1,2]{1,0:T(1,128)}, s32[1,2]{1,0:T(1,128)S(1)}, u32[]{:S(2)}) copy-start(s32[1,2]{1,0:T(1,128)S(1)} %collective-permute-done.links) | copy-start | bytes 28
  76.5 1.0 copy-start.1

commit v4 on v3

--- a/solution.py
+++ b/solution.py
@@ -28,9 +28,9 @@
     return slab * count + (index if slab % 2 == 0 else count - 1 - index)
 
 
-def pick_kernel(blocks, lists, counts, anom, innov, first, second, wide):
+def pick_kernel(blocks, lists, counts, anom, innov, out, wide):
     width, patches = lists.shape
-    members = first.shape[1]
+    members = out.shape[2]
     block = anom.shape[1]
     wide[0] = anom[...].astype(F32)
     wide[1] = innov[...].astype(F32)
@@ -40,9 +40,9 @@
         for j in range(width):
             entry = lists[j, p]
             keep = (j < counts[p]).astype(F32)
-            for kind, out in enumerate((first, second)):
+            for kind in range(2):
                 rows = wide[kind, pl.ds(entry, members, stride=blocks), :]
-                out[slot, :, j * block:(j + 1) * block] = (rows * keep).astype(BF16)
+                out[slot, kind, :, j * block:(j + 1) * block] = (rows * keep).astype(BF16)
         return carry
 
     lax.fori_loop(0, patches, patch, 0)
@@ -53,19 +53,21 @@
     patches, width = lists.shape
     return pl.pallas_call(
         functools.partial(pick_kernel, blocks),
-        out_shape=[jax.ShapeDtypeStruct((patches, members, width * block), BF16)] * 2,
+        out_shape=jax.ShapeDtypeStruct((patches, 2, members, width * block), BF16),
         in_specs=[SMEM_SPEC, SMEM_SPEC, VMEM_SPEC, VMEM_SPEC],
-        out_specs=[VMEM_SPEC] * 2,
+        out_specs=VMEM_SPEC,
         scratch_shapes=[pltpu.VMEM((2, members * blocks, block), F32)],
     )(lists.T, counts, anom.reshape(-1, block), innov.reshape(-1, block))
 
 
-def weight_kernel(anom, weight, a_ref, x_ref, w_ref):
-    members, size = anom.shape
+def weight_kernel(yz, weight, a_ref, x_ref, w_ref):
+    n, _, part, size = yz.shape
+    members = n * part
     shift = members - 1.0
+    anom = yz[:, 0].reshape(members, size)
     diag = lax.broadcasted_iota(jnp.int32, (size, size), 0) == lax.broadcasted_iota(jnp.int32, (size, size), 1)
     eye = jnp.where(diag, 1.0, 0.0).astype(F32)
-    a = mm(anom[...], anom[...], ((0,), (0,))) + shift * eye
+    a = mm(anom, anom, ((0,), (0,))) + shift * eye
     a_ref[...] = a
     bound = jnp.max(jnp.sum(jnp.abs(a), axis=0, keepdims=True))
     start = 2.0 / (shift + bound)
@@ -119,20 +121,21 @@
         weight[1, i * step:(i + 1) * step, :] = (w - wh.astype(F32)).astype(BF16)
 
 
-def patch_weight(anom):
-    members, size = anom.shape
+def patch_weight(yz):
+    n, _, part, size = yz.shape
+    members = n * part
     return pl.pallas_call(
         weight_kernel,
         out_shape=jax.ShapeDtypeStruct((2, members, size), BF16),
         in_specs=[VMEM_SPEC],
         out_specs=VMEM_SPEC,
         scratch_shapes=[pltpu.VMEM((size, size), F32)] * 3,
-        cost_estimate=pl.CostEstimate(flops=20 * 10**9, bytes_accessed=4 * 10**6, transcendentals=0),
-    )(anom)
-
-
-def update_kernel(n, slabs, links, weight, innov, states, out, prior, own, before, after, ready,
-                  send_f, recv_f, send_g, recv_g, send_d, recv_d, local_sem):
+        cost_estimate=pl.CostEstimate(flops=40 * 10**9, bytes_accessed=4 * 10**6, transcendentals=0),
+    )(yz)
+
+
+def update_kernel(n, slabs, links, weight, innov, prior, out, own, before, after, ready,
+                  send_g, recv_g, send_d, recv_d, local_sem):
     me, slab = lax.axis_index("mem"), lax.axis_index("slab")
     members, points = prior.shape
     part = members // n
@@ -164,9 +167,6 @@
 
     pl.semaphore_wait(barrier, n - 1 + edge_next + edge_prev)
 
-    def span(d):
-        return pl.ds(pl.multiple_of(d * part, part), part)
-
     def remote(src, dst, send, recv, device):
         return pltpu.make_async_remote_copy(
             src_ref=src, dst_ref=dst, send_sem=send, recv_sem=recv, device_id=device, device_id_type=MESH)
@@ -179,19 +179,6 @@
         side = mine + (1 - near) * (1 - 2 * mine)
         return side * half + lax.rem(place + s + near, half)
 
-    def send_states(s, carry):
-        c = far_first(s)
-        for i in range(inside):
-            d = c * inside + i
-
-            @pl.when(d != me)
-            def _():
-                remote(states.at[d], prior.at[span(me)], send_f.at[d], recv_f.at[me], peer(d)).start()
-        return carry
-
-    lax.fori_loop(0, chunks, send_states, 0)
-    prior[span(me), :] = states[me]
-
     def to_next(c):
         return remote(own.at[c], before.at[c], send_g.at[0, c], recv_g.at[0, c], following)
 
@@ -200,7 +187,7 @@
 
     def gains(s, carry):
         c = far_first(s)
-        rows = innov[pl.ds(pl.multiple_of(c * chunk, chunk), chunk), :]
+        rows = innov[pl.ds(c * (chunk // part), chunk // part), 1].reshape(chunk, innov.shape[-1])
         own[c] = (mm(weight[0], rows, ((1,), (1,))) + mm(weight[1], rows, ((1,), (1,)))).astype(BF16)
 
         @pl.when(has_next)
@@ -225,13 +212,6 @@
     up = 0.5 + 0.5 * links[0, 0].astype(F32)
     low = 0.5 + 0.5 * links[0, 1].astype(F32)
     scale = 1.0 + up + low
-
-    def states_came(s, carry):
-        d = lax.rem(me + s, n)
-        remote(states.at[d], prior.at[span(d)], send_f.at[d], recv_f.at[d], peer(d)).wait()
-        return carry
-
-    lax.fori_loop(1, n, states_came, 0)
 
     def copy(d):
         return remote(ready.at[d], out.at[row], send_d.at[d], recv_d.at[me], peer(d))
@@ -277,9 +257,9 @@
     keep.wait()
 
 
-def update(links, weight, innov, states, slabs):
-    n, part, points = states.shape
-    members = n * part
+def update(links, weight, innov, prior, n, slabs):
+    members, points = prior.shape
+    part = members // n
     chunk = max(part, min(128, members))
     gains = pltpu.VMEM((members // chunk, members, chunk), BF16)
     return pl.pallas_call(
@@ -287,14 +267,13 @@
         out_shape=jax.ShapeDtypeStruct((n, part, points), BF16),
         in_specs=[SMEM_SPEC] + [VMEM_SPEC] * 3,
         out_specs=ANY_SPEC,
-        scratch_shapes=[pltpu.VMEM((members, points), BF16), gains, gains, gains, pltpu.VMEM((n, part, points), BF16)]
-        + [pltpu.SemaphoreType.DMA((n,))] * 2
+        scratch_shapes=[gains, gains, gains, pltpu.VMEM((n, part, points), BF16)]
         + [pltpu.SemaphoreType.DMA((2, members // chunk))] * 2
         + [pltpu.SemaphoreType.DMA((n,))] * 2
         + [pltpu.SemaphoreType.DMA],
         compiler_params=pltpu.CompilerParams(collective_id=0, has_side_effects=True),
         cost_estimate=pl.CostEstimate(flops=2 * members * members * points, bytes_accessed=10**7, transcendentals=0),
-    )(links, weight, innov, states)
+    )(links, weight, innov, prior)
 
 
 def shifted(x, axis, by):
@@ -323,14 +302,10 @@
     swap = functools.partial(lax.all_to_all, axis_name="mem", split_axis=0, concat_axis=0, tiled=True)
     slabs = lax.axis_size("slab")
     links = lax.ppermute(patch_links, ("slab", "mem"), [(i, holder(i, n)) for i in range(slabs * n)])
-    anom, innov = pick(obs_anomalies, innovations, block_lists, block_counts)
-    states = forecast(ensemble, diffusivity, zonal_velocity)
-    anom = swap(anom)
-    anom, innov = lax.optimization_barrier((anom, innov))
-    innov = swap(innov)
-    size = anom.shape[-1]
-    weight = patch_weight(anom.reshape(-1, size))
-    out = update(links, weight, innov.reshape(-1, size), states, slabs)
+    yz = swap(pick(obs_anomalies, innovations, block_lists, block_counts))
+    prior = swap(forecast(ensemble, diffusivity, zonal_velocity))
+    weight = patch_weight(yz)
+    out = update(links, weight, yz, prior.reshape(-1, prior.shape[-1]), n, slabs)
     return jnp.transpose(out, (1, 0, 2))
 
 

time: 223 us -> 195 us (0.87)
  the two profiles are of different devices: /device:TPU:5 before, /device:TPU:0 now
where the time goes in v4:
time: 195 us; the launch traced here: 192 us
  Pallas kernels  98.9 us (51%)
  waiting for transfers between devices  61.1 us (31%)
  starting transfers between devices  15.5 us (8%)
  local copies, waits for them, and re-layouts  10.4 us (5%)
  other arithmetic  5.95 us (3%)
    pallas_call x1, Pallas kernels, update(): pl.pallas_call(functools.partial(update_kernel, n, slabs), out_shape=jax....  73.3 us
    all_to_all x1, waiting for transfers between devices, local(): prior = swap(forecast(ensemble, diffusivity, zonal_velocity))  28.4 us
    all_to_all x1, waiting for transfers between devices, local(): yz = swap(pick(obs_anomalies, innovations, block_lists, block_counts))  21.3 us
    pallas_call x1, Pallas kernels, patch_weight(): pl.pallas_call(weight_kernel, out_shape=jax.ShapeDtypeStruct((2, members,...  20.6 us
    ppermute x2, waiting for transfers between devices, shifted(): return lax.ppermute(x, axis, pairs)  11.4 us
    all_to_all x1, starting transfers between devices, local(): yz = swap(pick(obs_anomalies, innovations, block_lists, block_counts))  6.5 us
    pallas_call x1, Pallas kernels, pick(): pl.pallas_call(functools.partial(pick_kernel, blocks), out_shape=jax.Shap...  4.99 us
    ppermute x2, starting transfers between devices, shifted(): return lax.ppermute(x, axis, pairs)  4.7 us
  transfers between devices with their start and end apart: 5, of which 4 were waited for; matrix products, arithmetic and copies ran while one was open for 6% of the time, Pallas kernels for 11%

profile of v4, /device:TPU:0, one launch (start us, length us, event | category | flops | bytes accessed | tf_op | source)
XLA Modules:
  0.0 191.9 jit_solution(6385695193365717203)
XLA Ops:
  0.0 5.0 %shard_map.82 = bf16[8,2,128,512]{3,2,1,0:T(8,128)(2,1)} custom-call(s32[4,8]{1,0:T(4,128)} %bitcast.14, s32[8]{0:T(128)} %counts.1, bf16[2048,128]{1,0:T(8,128)(2,1)} %bitcast.12, bf16[2048,128]{1,0:T(8,128)(2,1)} %bitcast.13), custom_call_target="tpu_custom_call" | custom-call | tf_op jit(solution)/shard_map/pallas_call | solution.py:54
  5.0 0.0 copy-start.4
  5.0 0.0 copy-start.2
  5.0 0.0 copy-start.1
  5.0 6.5 %all-to-all-start = ((bf16[8,2,128,512]{3,2,1,0:T(8,128)(2,1)}), bf16[8,2,128,512]{3,2,1,0:T(8,128)(2,1)}, u32[]{:S(2)}, u32[]{:S(2)}) async-start(bf16[8,2,128,512]{3,2,1,0:T(8,128)(2,1)} %shard_map.82), calls=%async_computation | async-start | bytes 4194304 | tf_op jit(solution)/shard_map/all_to_all | solution.py:305
  11.5 2.7 %copy.14 = bf16[128,8,1024]{2,0,1:T(8,128)(2,1)S(1)} copy(bf16[128,8,1024]{2,1,0:T(8,128)(2,1)} %param.8) | data formatting | bytes 4194304 | tf_op args[0]
  14.3 3.4 %collective-permute-start.1 = (bf16[1,128,1024]{2,1,0:T(8,128)(2,1)S(1)}, bf16[1,128,1024]{2,1,0:T(8,128)(2,1)S(1)}, u32[]{:S(2)}, u32[]{:S(2)}) collective-permute-start(bf16[1,128,1024]{2,1,0:T(8,128)(2,1)S(1)} %get-tuple-element.9), channel_id=1, source_target_pairs={{0,8},{8,16},{16,24},{1,9},{9,17},{17,25},{2,10},{10,18},{18,26},{... | collective-permute-start | bytes 786440 | tf_op jit(solution)/shard_map/ppermute | solution.py:282
  17.7 1.3 collective-permute-start.2
  19.0 0.0 copy-done.4
  19.0 0.7 collective-permute-start
  19.7 0.0 copy-done.2
  19.7 0.2 rev.10
  19.9 0.0 copy-done.1
  19.9 0.2 rev.11
  20.1 3.9 %collective-permute-done.1 = bf16[1,128,1024]{2,1,0:T(8,128)(2,1)S(1)} collective-permute-done((bf16[1,128,1024]{2,1,0:T(8,128)(2,1)S(1)}, bf16[1,128,1024]{2,1,0:T(8,128)(2,1)S(1)}, u32[]{:S(2)}, u32[]{:S(2)}) %collective-permute-start.1) | collective-permute-done | bytes 262176 | tf_op jit(solution)/shard_map/ppermute | solution.py:282
  23.9 7.6 %collective-permute-done.2 = bf16[1,128,1024]{2,1,0:T(8,128)(2,1)S(1)} collective-permute-done((bf16[1,128,1024]{2,1,0:T(8,128)(2,1)S(1)}, bf16[1,128,1024]{2,1,0:T(8,128)(2,1)S(1)}, u32[]{:S(2)}, u32[]{:S(2)}) %collective-permute-start.2) | collective-permute-done | bytes 262176 | tf_op jit(solution)/shard_map/ppermute | solution.py:282
  31.5 0.3 pad_maximum_fusion.2
  31.8 0.8 reverse_select_fusion
  32.6 0.5 slice_convert_fusion
  33.1 0.2 fusion.1
  33.3 1.7 fusion
  35.0 4.4 %add_convert_fusion = bf16[8,128,1024]{2,1,0:T(8,128)(2,1)} fusion(f32[8,128,1023]{2,1,0:T(8,128)S(1)} %get-tuple-element.6, f32[8,128,1]{2,1,0:T(8,128)S(1)} %get-tuple-element.8, f32[8,128,1]{2,1,0:T(8,128)S(1)} %get-tuple-element.7, f32[8,128,1023]{2,1,0:T(8,128)S(1)} %get-tuple-element.5, bf16[10,128,1024]{2,1,0:T(8,128)(2,1)S(1)} %reverse_select_fusion, ...), kind=kLoop, calls=%fused_computation.2 | loop fusion | flops 17825792 | bytes 16842752 | tf_op jit(solution)/shard_map/convert_element_type | solution.py:297
  39.3 21.3 %all-to-all-done.yz.innov = bf16[8,2,128,512]{3,2,1,0:T(8,128)(2,1)} async-done(((bf16[8,2,128,512]{3,2,1,0:T(8,128)(2,1)}), bf16[8,2,128,512]{3,2,1,0:T(8,128)(2,1)}, u32[]{:S(2)}, u32[]{:S(2)}) %all-to-all-start) | async-done | bytes 2097184 | tf_op jit(solution)/shard_map/all_to_all | solution.py:305
  60.6 3.6 %all-to-all-start.1 = ((bf16[8,128,1024]{2,1,0:T(8,128)(2,1)}), bf16[8,128,1024]{2,1,0:T(8,128)(2,1)S(1)}, u32[]{:S(2)}, u32[]{:S(2)}) async-start(bf16[8,128,1024]{2,1,0:T(8,128)(2,1)} %add_convert_fusion), calls=%async_computation.1 | async-start | bytes 4194304 | tf_op jit(solution)/shard_map/all_to_all | solution.py:306
  64.3 20.6 %shard_map.83.weight = bf16[2,1024,512]{2,1,0:T(8,128)(2,1)} custom-call(bf16[8,2,128,512]{3,2,1,0:T(8,128)(2,1)} %all-to-all-done.yz.innov), custom_call_target="tpu_custom_call" | custom-call | flops 40000000000 | bytes 4000000 | tf_op jit(solution)/shard_map/pallas_call | solution.py:127
  84.8 0.0 collective-permute-done.links
  84.8 0.0 copy-start.3
  84.8 28.4 %all-to-all-done.1 = bf16[8,128,1024]{2,1,0:T(8,128)(2,1)S(1)} async-done(((bf16[8,128,1024]{2,1,0:T(8,128)(2,1)}), bf16[8,128,1024]{2,1,0:T(8,128)(2,1)S(1)}, u32[]{:S(2)}, u32[]{:S(2)}) %all-to-all-start.1) | async-done | bytes 2097184 | tf_op jit(solution)/shard_map/all_to_all | solution.py:306
  113.2 0.0 copy-start
  113.2 0.0 copy-done.3
  113.2 1.3 copy-done
  114.5 73.3 %shard_map.84 = bf16[8,128,1024]{2,1,0:T(8,128)(2,1)} custom-call(s32[1,2]{1,0:T(1,128)} %copy-done.3, bf16[2,1024,512]{2,1,0:T(8,128)(2,1)} %shard_map.83.weight, bf16[8,2,128,512]{3,2,1,0:T(8,128)(2,1)} %all-to-all-done.yz.innov, bf16[1024,1024]{1,0:T(8,128)(2,1)} %bitcast.10), custom_call_target="tpu_custom_call" | custom-call | flops 2147483648 | bytes 10000000 | tf_op jit(solution)/shard_map/pallas_call | solution.py:265
  187.8 4.1 %copy.12 = bf16[128,8,1024]{2,1,0:T(8,128)(2,1)} copy(bf16[128,8,1024]{2,0,1:T(8,128)(2,1)} %bitcast.11) | data formatting | bytes 4194304 | tf_op jit(solution)/shard_map/transpose | solution.py:309
  (2 shorter events, 0.0 us)
Async XLA Ops:
  5.0 14.0 %copy-start.4 = (s32[1,2]{1,0:T(1,128)S(1)}, s32[1,2]{1,0:T(1,128)}, u32[]{:S(2)}) copy-start(s32[1,2]{1,0:T(1,128)} %param.15) | copy-start | bytes 28
  5.0 14.7 %copy-start.2 = (f32[8,1024]{1,0:T(8,128)S(1)}, f32[8,1024]{1,0:T(8,128)}, u32[]{:S(2)}) copy-start(f32[8,1024]{1,0:T(8,128)} %param.9) | copy-start | bytes 98308
  5.0 14.9 %copy-start.1 = (f32[8,1024]{1,0:T(8,128)S(1)}, f32[8,1024]{1,0:T(8,128)}, u32[]{:S(2)}) copy-start(f32[8,1024]{1,0:T(8,128)} %param.10) | copy-start | bytes 98308
  5.0 55.6 %all-to-all-start = ((bf16[8,2,128,512]{3,2,1,0:T(8,128)(2,1)}), bf16[8,2,128,512]{3,2,1,0:T(8,128)(2,1)}, u32[]{:S(2)}, u32[]{:S(2)}) async-start(bf16[8,2,128,512]{3,2,1,0:T(8,128)(2,1)} %shard_map.82), calls=%async_computation | async-start | bytes 4194304 | tf_op jit(solution)/shard_map/all_to_all | solution.py:305
  14.3 9.6 %collective-permute-start.1 = (bf16[1,128,1024]{2,1,0:T(8,128)(2,1)S(1)}, bf16[1,128,1024]{2,1,0:T(8,128)(2,1)S(1)}, u32[]{:S(2)}, u32[]{:S(2)}) collective-permute-start(bf16[1,128,1024]{2,1,0:T(8,128)(2,1)S(1)} %get-tuple-element.9), channel_id=1, source_target_pairs={{0,8},{8,16},{16,24},{1,9},{9,17},{17,25},{2,10},{10,18},{18,26},{... | collective-permute-start | bytes 786440 | tf_op jit(solution)/shard_map/ppermute | solution.py:282
  17.7 13.8 %collective-permute-start.2 = (bf16[1,128,1024]{2,1,0:T(8,128)(2,1)S(1)}, bf16[1,128,1024]{2,1,0:T(8,128)(2,1)S(1)}, u32[]{:S(2)}, u32[]{:S(2)}) collective-permute-start(bf16[1,128,1024]{2,1,0:T(8,128)(2,1)S(1)} %get-tuple-element.10), channel_id=1, source_target_pairs={{8,0},{16,8},{24,16},{9,1},{17,9},{25,17},{10,2},{18,10},{26,18},{... | collective-permute-start | bytes 786440 | tf_op jit(solution)/shard_map/ppermute | solution.py:282
  19.0 65.8 %collective-permute-start = (s32[1,2]{1,0:T(1,128)S(1)}, s32[1,2]{1,0:T(1,128)S(1)}, u32[]{:S(2)}, u32[]{:S(2)}) collective-permute-start(s32[1,2]{1,0:T(1,128)S(1)} %copy-done.4), channel_id=1, source_target_pairs={{0,0},{1,1},{2,2},{3,3},{4,4},{5,5},{6,6},{7,7},{8,15},{9,14},{10,... | collective-permute-start | bytes 32 | tf_op jit(solution)/shard_map/ppermute | solution.py:304
  60.6 52.6 %all-to-all-start.1 = ((bf16[8,128,1024]{2,1,0:T(8,128)(2,1)}), bf16[8,128,1024]{2,1,0:T(8,128)(2,1)S(1)}, u32[]{:S(2)}, u32[]{:S(2)}) async-start(bf16[8,128,1024]{2,1,0:T(8,128)(2,1)} %add_convert_fusion), calls=%async_computation.1 | async-start | bytes 4194304 | tf_op jit(solution)/shard_map/all_to_all | solution.py:306
  84.8 28.4 %copy-start.3 = (s32[1,2]{1,0:T(1,128)}, s32[1,2]{1,0:T(1,128)S(1)}, u32[]{:S(2)}) copy-start(s32[1,2]{1,0:T(1,128)S(1)} %collective-permute-done.links) | copy-start | bytes 28
  113.2 1.3 copy-start
